TPU v7x, 256 devices: a whole 4x4x8 slice. The times are simulated.
256 devices in a mesh: row: 8 (over x, core), col: 32 (over z, y).
Axes of the slice: x: 4, y: 4, z: 8, core: 2. Of those that a mesh axis runs over, the one named last changes fastest.
Arguments:
- features: float32 [32768, 512], P(('col', 'row')), may hold values from -6 to 6
- weight: float32 [512, 512], replicated, may hold values from -0.25 to 0.25
- cotangent: bfloat16 [32768, 512], P(('row', 'col')), may hold values from -6 to 6
- block_values: bfloat16 [8, 32, 96, 128, 128], P('row', 'col'), may hold values from -0.0625 to 0.0625
- block_coords: int32 [8, 32, 2, 96], P('row', 'col'), may hold values from -1 to 31, as said below
Outputs:
- activated: float32 [32768, 512], P(('row', 'col'))
- dfeatures: float32 [32768, 512], P(('col', 'row'))
- dweight: float32 [512, 512], P('row', 'col')
Inputs may be any that keep to these rules, and one draw needn't show every extreme that they name: block_coords[r, c, 0, s] is a block row below 32 and block_coords[r, c, 1, s] a block column below 8 of slot s of device (r, c), or both are -1 for an unused slot. Used slots come first and name distinct blocks; each device uses between a quarter of 96 (rounded down) and all 96 slots, and some device uses all 96.
All inputs are finite; a program needn't handle non-finite values.
Results may differ from a plain program's by a relative error of at most 0.006.
Values may be sent and summed in bfloat16 or wider, within the bound.
No kernel may reach another device: no remote copies, remote signals or barrier semaphores. Data moves between devices by JAX's collectives and lax.ppermute only.
A program may use at most 128 MiB of HBM per device.

v0:
```python
import jax
import jax.numpy as jnp
from jax import lax
from jax.experimental import pallas as pl
from jax.experimental.pallas import tpu as pltpu
from jax.sharding import PartitionSpec as P

HID = 512
BLK = 128
NB = 96
NX, NC, NZ, NY = 4, 2, 8, 4
HALF = BLK // 2
TOP = 80
PIECES = 2
F32 = jnp.float32
BF16 = jnp.bfloat16


def shift(value, axis, step):
    if axis == "z":
        return lax.ppermute(
            value, "col", [(i, (i // NY + step) % NZ * NY + i % NY) for i in range(NZ * NY)]
        )
    if axis == "y":
        return lax.ppermute(
            value, "col", [(i, i // NY * NY + (i % NY + step) % NY) for i in range(NZ * NY)]
        )
    if axis == "x":
        return lax.ppermute(
            value, "row", [(i, (i // NC + step) % NX * NC + i % NC) for i in range(NX * NC)]
        )
    return lax.ppermute(value, "row", [(i, i ^ 1) for i in range(NX * NC)])


def ring_sum(chunks, axis, cut=None, wire=BF16):
    count = len(chunks)
    far = count // 2
    cut = cut or chunks[0].shape[0] // 2

    def both_ways(right, left):
        right = shift(right.astype(wire), axis, 1).astype(F32)
        left = shift(left.astype(wire), axis, -1).astype(F32)
        return right, left

    right, left = both_ways(chunks[far][:cut], chunks[far][cut:])
    for d in range(far - 1, 0, -1):
        ahead, behind = chunks[d].astype(F32), chunks[count - d].astype(F32)
        if d == far - 1:
            ahead = jnp.concatenate([ahead[:cut] + right, ahead[cut:]], 0)
            behind = jnp.concatenate([behind[:cut], behind[cut:] + left], 0)
        else:
            ahead = ahead + right
            behind = behind + left
        right, left = both_ways(ahead, behind)
    own = chunks[0].astype(F32)
    return own + right + left


def ring_gather(own, axis, count):
    pieces = [None] * count
    pieces[0] = right = left = own
    for step in range(1, count // 2 + 1):
        right = shift(right, axis, 1)
        pieces[count - step] = right
        if step < count - step:
            left = shift(left, axis, -1)
            pieces[step] = left
    return pieces


def fill_tile(slot, vals_ref, lhs_ref, row, col):
    tile = vals_ref[jnp.minimum(slot, NB - 1)]
    lhs_ref[pl.ds(row, BLK), pl.ds(col, BLK)] = jnp.where(
        slot < NB, tile, jnp.zeros_like(tile)
    )


def whole(*shape):
    return pl.BlockSpec(shape, lambda *_: (0,) * len(shape), pipeline_mode=pl.Buffered(1))


def forward_kernel(table, place, vals, *rest):
    pieces = rest[:PIECES]
    y0, y1, y2, y3, zo, gathered, lhs, sems = rest[PIECES:]
    turn = pl.program_id(0)

    def tile_rows(turn):
        for k in range(NY):
            for j in range(NX * NC):
                slot = table[(turn * NY + k) * NX * NC + j]
                fill_tile(slot, vals, lhs, k * BLK, j * BLK)

    @pl.when(turn == 0)
    def _():
        copies, start = [], 0
        for k, piece in enumerate(pieces):
            count = piece.shape[0]
            copies.append(
                pltpu.make_async_copy(piece, gathered.at[pl.ds(start, count)], sems.at[k])
            )
            start += count
        for copy in copies:
            copy.start()
        for copy in copies:
            copy.wait()

    tile_rows(turn)
    out = jnp.dot(lhs[...], gathered[...], preferred_element_type=F32).astype(BF16)
    for k, y in enumerate((y0, y1, y2, y3)):
        y[0] = out[k * BLK : k * BLK + TOP]
        zo[0, k] = out[k * BLK + TOP : (k + 1) * BLK]


def forward_blocks(table, place, vals, pieces):
    yspec = pl.BlockSpec((1, TOP, HID), lambda g, t, p: (lax.rem(g + p[0], NZ), 0, 0))
    nodes = NX * NC * BLK
    return pl.pallas_call(
        forward_kernel,
        grid_spec=pltpu.PrefetchScalarGridSpec(
            num_scalar_prefetch=2,
            grid=(NZ,),
            in_specs=[whole(NB, BLK, BLK)] + [pl.BlockSpec(memory_space=pltpu.HBM)] * len(pieces),
            out_specs=[yspec] * NY
            + [pl.BlockSpec((1, NY, BLK - TOP, HID), lambda g, t, p: (g, 0, 0, 0))],
            scratch_shapes=[
                pltpu.VMEM((nodes, HID), BF16),
                pltpu.VMEM((NY * BLK, nodes), BF16),
                pltpu.SemaphoreType.DMA((len(pieces),)),
            ],
        ),
        out_shape=[jax.ShapeDtypeStruct((NZ, TOP, HID), BF16)] * NY
        + [jax.ShapeDtypeStruct((NZ, NY, BLK - TOP, HID), BF16)],
        compiler_params=pltpu.CompilerParams(vmem_limit_bytes=16 << 20),
        name="forward_blocks",
    )(table, place, vals, *pieces)


def turn_kernel(after, vals, vals_t):
    del after
    for k in range(vals.shape[0]):
        vals_t[k] = vals[k].T


def turned(vals, after):
    group = 12
    block = pl.BlockSpec((group, BLK, BLK), lambda g: (g, 0, 0))
    return pl.pallas_call(
        turn_kernel,
        grid=(NB // group,),
        in_specs=[pl.BlockSpec(memory_space=pl.ANY), block],
        out_specs=block,
        out_shape=jax.ShapeDtypeStruct((NB, BLK, BLK), BF16),
        compiler_params=pltpu.CompilerParams(vmem_limit_bytes=4 << 20),
        name="turned",
    )(after, vals)


def backward_kernel(table, place, vals, *rest):
    pieces = rest[: NY + NZ]
    near, away, slope, acc, lhs, sems = rest[NY + NZ :]
    turn = pl.program_id(0)

    @pl.when(turn == 0)
    def _():
        lower, upper = pl.ds(0, HALF), pl.ds(HALF, HALF)
        moves = [(pieces[k], slope.at[:, k, lower]) for k in range(NY)]
        for k in range(NZ):
            moves.append((pieces[NY + k], slope.at[lax.rem(place[0] + k, NZ), :, upper]))
        copies = [
            pltpu.make_async_copy(src, dst, sems.at[k]) for k, (src, dst) in enumerate(moves)
        ]
        for copy in copies:
            copy.start()
        acc[...] = jnp.zeros_like(acc)
        for copy in copies:
            copy.wait()

    for j in range(NX * NC):
        for k in range(NY):
            slot = table[(turn * NY + k) * NX * NC + j]
            fill_tile(slot, vals, lhs, j * BLK, k * BLK)

    acc[...] += jnp.dot(
        lhs[...], slope[turn].reshape(NY * BLK, HID), preferred_element_type=F32
    )

    @pl.when(turn == NZ - 1)
    def _():
        near[...] = acc[: NX * BLK]
        away[...] = acc[NX * BLK :].astype(BF16)


def backward_blocks(table, place, vals, pieces):
    nodes = NX * NC * BLK
    return pl.pallas_call(
        backward_kernel,
        grid_spec=pltpu.PrefetchScalarGridSpec(
            num_scalar_prefetch=2,
            grid=(NZ,),
            in_specs=[whole(NB, BLK, BLK)] + [pl.BlockSpec(memory_space=pltpu.HBM)] * len(pieces),
            out_specs=[whole(NX * BLK, HID), whole(NX * BLK, HID)],
            scratch_shapes=[
                pltpu.VMEM((NZ, NY, BLK, HID), BF16),
                pltpu.VMEM((nodes, HID), F32),
                pltpu.VMEM((nodes, NY * BLK), BF16),
                pltpu.SemaphoreType.DMA((len(pieces),)),
            ],
        ),
        out_shape=[
            jax.ShapeDtypeStruct((NX * BLK, HID), F32),
            jax.ShapeDtypeStruct((NX * BLK, HID), BF16),
        ],
        compiler_params=pltpu.CompilerParams(vmem_limit_bytes=20 << 20),
        name="backward_blocks",
    )(table, place, vals, *pieces)


def slot_table(block_rows, block_cols, live):
    key = jnp.where(live, block_rows * (NX * NC) + block_cols, -1)
    shape = (NZ * NY * NX * NC, NB)
    spots = lax.broadcasted_iota(jnp.int32, shape, 0)
    slot_ids = lax.broadcasted_iota(jnp.int32, shape, 1)
    return jnp.min(jnp.where(spots == key[None, :], slot_ids, NB), axis=1)


ZGROUPS = [[k * NY + n for k in range(NZ)] for n in range(NY)]


def exchange(parts, groups):
    return lax.all_to_all(parts, "col", 0, 0, axis_index_groups=groups, tiled=True)


def spread(own, groups):
    return exchange(jnp.broadcast_to(own, (len(groups[0]), *own.shape)), groups)


def on_device(features, weight, cotangent, block_values, block_coords):
    values = block_values[0, 0]
    coords = block_coords[0, 0]
    row = lax.axis_index("row")
    col = lax.axis_index("col")
    x, core = row // NC, row % NC
    z, y = col // NY, col % NY
    place = jnp.stack([z, y]).astype(jnp.int32)

    near_x = jnp.concatenate(ring_gather(features.astype(BF16), "x", NX), 0)
    gathered = [near_x, shift(near_x, "core", 1)]

    live = coords[0] >= 0
    zr = lax.rem(coords[0] // NY - z + NZ, NZ)
    yr = lax.rem(coords[0] % NY - y + NY, NY)
    xr = lax.rem(coords[1] // NC - x + NX, NX)
    cr = lax.rem(coords[1] % NC - core + NC, NC)
    forward_table = slot_table(zr * NY + yr, cr * NX + xr, live)
    backward_table = slot_table(coords[0] // NY * NY + yr, cr * NX + xr, live)

    y0, y1, y2, y3, zo = forward_blocks(forward_table, place, values, gathered)
    values_t = turned(values, zo)
    by_y = ring_sum([y0, y1, y2, y3], "y").astype(BF16)
    by_z = ring_sum([zo[k] for k in range(NZ)], "z")
    top = exchange(by_y, ZGROUPS)
    bottom = ring_sum([by_z[k] for k in range(NY)], "y", wire=F32)
    top = jnp.sum(top.astype(F32), axis=0)
    mixed = jnp.concatenate([top, bottom], 0)

    wcopy = weight.astype(BF16)
    high = mixed.astype(BF16)
    low = (mixed - high.astype(F32)).astype(BF16)
    total = jnp.dot(high, wcopy, preferred_element_type=F32)
    total = total + jnp.dot(low, wcopy, preferred_element_type=F32)
    sigma = jax.nn.sigmoid(total)
    activated = total * sigma
    slope = cotangent.astype(F32) * sigma * (1.0 + total * (1.0 - sigma))
    slope = slope.astype(BF16)

    top_all = spread(slope[:HALF], ZGROUPS)
    bottom_all = jnp.stack(ring_gather(slope[HALF:], "y", NY))
    ypieces = ring_gather(top_all, "y", NY)
    zpieces = ring_gather(bottom_all, "z", NZ)
    pieces = ypieces + zpieces

    part, width = HID // (NX * NC), HID // (NZ * NY)
    pull = lambda left: lax.dot_general(
        slope, left, (((0,), (0,)), ((), ())), preferred_element_type=F32
    )
    local = (pull(high) + pull(low)).astype(BF16).reshape(NZ * NY, width, HID)
    shares = lax.all_to_all(local, "col", 0, 0, tiled=True)
    shares = jnp.sum(shares.astype(F32), axis=0).reshape(width, NX, NC, part)
    shares = shares.transpose(1, 2, 0, 3).reshape(NX, NC, width * part // HID, HID)
    shares = lax.dynamic_slice_in_dim(jnp.concatenate([shares, shares], 0), x, NX, 0)
    mine = lax.dynamic_index_in_dim(shares, core, 1, keepdims=False)
    other = lax.dynamic_index_in_dim(shares, 1 - core, 1, keepdims=False)
    mine = mine + shift(other, "core", 1)

    near, away = backward_blocks(backward_table, place, values_t, pieces)
    near = near + shift(away, "core", 1).astype(F32)
    spare = jnp.zeros((NX, 16 - mine.shape[1], HID), F32)
    both = jnp.concatenate([near.reshape(NX, BLK, HID), mine, spare], 1)
    sums = ring_sum([both[k] for k in range(NX)], "x", 80)
    grad = sums[:BLK].astype(BF16)
    dfeatures = lax.dot_general(
        grad, wcopy, (((1,), (1,)), ((), ())), preferred_element_type=F32
    )
    node_total = BLK * NX * NC * NZ * NY
    dweight = sums[BLK : BLK + mine.shape[1]].reshape(width, part).T * (1.0 / node_total**0.5)
    return activated, dfeatures, dweight


def solution(mesh):
    placed = (
        P(("col", "row"), None),
        P(),
        P(("row", "col"), None),
        P("row", "col", None, None, None),
        P("row", "col", None, None),
    )

    return jax.shard_map(
        on_device,
        mesh=mesh,
        in_specs=placed,
        out_specs=(P(("row", "col"), None), P(("col", "row"), None), P("row", "col")),
        check_vma=False,
    )
```

profile of v0, /device:TPU:8, one launch (start us, length us, event | category | flops | bytes accessed | tf_op | source)
XLA Modules:
  0.0 189.0 jit_solution(2831711166952016395)
XLA Ops:
  4.9 3.2 %collective-permute-done.1 = bf16[128,512]{1,0:T(8,128)(2,1)S(1)} collective-permute-done((bf16[128,512]{1,0:T(8,128)(2,1)S(1)}, bf16[128,512]{1,0:T(8,128)(2,1)S(1)}, u32[]{:S(2)}, u32[]{:S(2)}) %collective-permute-start.1) | collective-permute-done | bytes 131104 | tf_op jit(solution)/shard_map/ppermute | solution.py:29
  8.5 5.8 %collective-permute-done.2 = bf16[128,512]{1,0:T(8,128)(2,1)S(1)} collective-permute-done((bf16[128,512]{1,0:T(8,128)(2,1)S(1)}, bf16[128,512]{1,0:T(8,128)(2,1)S(1)}, u32[]{:S(2)}, u32[]{:S(2)}) %collective-permute-start.2) | collective-permute-done | bytes 131104 | tf_op jit(solution)/shard_map/ppermute | solution.py:29
  18.2 6.6 %forward_blocks.1 = (bf16[8,80,512]{2,1,0:T(8,128)(2,1)S(1)}, bf16[8,80,512]{2,1,0:T(8,128)(2,1)S(1)}, bf16[8,80,512]{2,1,0:T(8,128)(2,1)S(1)}, bf16[8,80,512]{2...) custom-call(s32[256]{0:T(256)S(1)} %select_reduce_fusion.1.table, s32[2]{0:T(128)S(1)} %pad_add_fusion.place, ...), custom_call_target="tpu_custom_call" | custom-call | tf_op jit(solution)/shard_map/forward_blocks/pallas_call | solution.py:117
  26.9 4.0 %collective-permute-start.12 = (bf16[2,48,512]{2,1,0:T(8,128)(2,1)S(1)}, bf16[2,48,512]{2,1,0:T(8,128)(2,1)S(1)}, u32[]{:S(2)}, u32[]{:S(2)}) collective-permute-start(bf16[2,48,512]{2,1,0:T(8,128)(2,1)S(1)} %get-tuple-element.26), channel_id=1, source_target_pairs={{0,28},{1,29},{2,30},{3,31},{4,0},{5,1},{6,2},{7,3},{8,4},{9,5},{1... | collective-permute-start | bytes 294920 | tf_op jit(solution)/shard_map/ppermute | solution.py:21
  30.9 3.0 %collective-permute-done.8 = bf16[2,48,512]{2,1,0:T(8,128)(2,1)S(1)} collective-permute-done((bf16[2,48,512]{2,1,0:T(8,128)(2,1)S(1)}, bf16[2,48,512]{2,1,0:T(8,128)(2,1)S(1)}, u32[]{:S(2)}, u32[]{:S(2)}) %collective-permute-start.8) | collective-permute-done | bytes 98336 | tf_op jit(solution)/shard_map/ppermute | solution.py:21
  36.4 3.3 %collective-permute-start.13 = (bf16[4,48,512]{2,1,0:T(8,128)(2,1)S(1)}, bf16[4,48,512]{2,1,0:T(8,128)(2,1)S(1)}, u32[]{:S(2)}, u32[]{:S(2)}) collective-permute-start(bf16[4,48,512]{2,1,0:T(8,128)(2,1)S(1)} %pad_maximum_fusion.6), channel_id=1, source_target_pairs={{0,28},{1,29},{2,30},{3,31},{4,0},{5,1},{6,2},{7,3},{8,4},{9,5},{1... | collective-permute-start | bytes 589832 | tf_op jit(solution)/shard_map/ppermute | solution.py:21
  50.9 4.2 %collective-permute-done.14 = bf16[4,48,512]{2,1,0:T(8,128)(2,1)S(1)} collective-permute-done((bf16[4,48,512]{2,1,0:T(8,128)(2,1)S(1)}, bf16[4,48,512]{2,1,0:T(8,128)(2,1)S(1)}, u32[]{:S(2)}, u32[]{:S(2)}) %collective-permute-start.14) | collective-permute-done | bytes 196640 | tf_op jit(solution)/shard_map/ppermute | solution.py:21
  56.2 2.8 %collective-permute-done.7 = bf16[8,80,512]{2,1,0:T(8,128)(2,1)S(1)} collective-permute-done((bf16[8,80,512]{2,1,0:T(8,128)(2,1)S(1)}, bf16[8,80,512]{2,1,0:T(8,128)(2,1)S(1)}, u32[]{:S(2)}, u32[]{:S(2)}) %collective-permute-start.7) | collective-permute-done | bytes 655392 | tf_op jit(solution)/shard_map/ppermute | solution.py:25
  59.0 2.9 %collective-permute-done.5 = bf16[8,80,512]{2,1,0:T(8,128)(2,1)S(1)} collective-permute-done((bf16[8,80,512]{2,1,0:T(8,128)(2,1)S(1)}, bf16[8,80,512]{2,1,0:T(8,128)(2,1)S(1)}, u32[]{:S(2)}, u32[]{:S(2)}) %collective-permute-start.5) | collective-permute-done | bytes 655392 | tf_op jit(solution)/shard_map/ppermute | solution.py:25
  63.0 5.0 %all-to-all-start = ((bf16[8,80,512]{2,1,0:T(8,128)(2,1)}), bf16[8,80,512]{2,1,0:T(8,128)(2,1)S(1)}, u32[]{:S(2)}, u32[]{:S(2)}) async-start(bf16[8,80,512]{2,1,0:T(8,128)(2,1)} %add_convert_fusion), calls=%async_computation | async-start | bytes 1310720 | tf_op jit(solution)/shard_map/all_to_all | solution.py:230
  68.2 3.0 %collective-permute-start.18 = (f32[24,512]{1,0:T(8,128)S(1)}, f32[24,512]{1,0:T(8,128)S(1)}, u32[]{:S(2)}, u32[]{:S(2)}) collective-permute-start(f32[24,512]{1,0:T(8,128)S(1)} %get-tuple-element.38), channel_id=1, source_target_pairs={{0,3},{1,0},{2,1},{3,2},{4,7},{5,4},{6,5},{7,6},{8,11},{9,8},{10,9... | collective-permute-start | bytes 147464 | tf_op jit(solution)/shard_map/ppermute | solution.py:25
  73.4 3.2 %collective-permute-start.19 = (f32[48,512]{1,0:T(8,128)S(1)}, f32[48,512]{1,0:T(8,128)S(1)}, u32[]{:S(2)}, u32[]{:S(2)}) collective-permute-start(f32[48,512]{1,0:T(8,128)S(1)} %pad_maximum_fusion.10), channel_id=1, source_target_pairs={{0,3},{1,0},{2,1},{3,2},{4,7},{5,4},{6,5},{7,6},{8,11},{9,8},{10,9... | collective-permute-start | bytes 294920 | tf_op jit(solution)/shard_map/ppermute | solution.py:25
  79.0 4.0 %collective-permute-done.17 = f32[48,512]{1,0:T(8,128)S(1)} collective-permute-done((f32[48,512]{1,0:T(8,128)S(1)}, f32[48,512]{1,0:T(8,128)S(1)}, u32[]{:S(2)}, u32[]{:S(2)}) %collective-permute-start.17) | collective-permute-done | bytes 98336 | tf_op jit(solution)/shard_map/ppermute | solution.py:25
  88.7 4.5 %all-to-all-start.1 = ((bf16[8,64,512]{2,1,0:T(8,128)(2,1)}), bf16[8,64,512]{2,1,0:T(8,128)(2,1)}, u32[]{:S(2)}, u32[]{:S(2)}) async-start(bf16[8,64,512]{2,1,0:T(8,128)(2,1)} %broadcast_in_dim.17), calls=%async_computation.1 | async-start | bytes 1048576 | tf_op jit(solution)/shard_map/all_to_all | solution.py:230
  93.5 3.3 %collective-permute-start.23 = (bf16[64,512]{1,0:T(8,128)(2,1)}, bf16[64,512]{1,0:T(8,128)(2,1)}, u32[]{:S(2)}, u32[]{:S(2)}) collective-permute-start(bf16[64,512]{1,0:T(8,128)(2,1)} %get-tuple-element.44), channel_id=1, source_target_pairs={{0,3},{1,0},{2,1},{3,2},{4,7},{5,4},{6,5},{7,6},{8,11},{9,8},{10,9... | collective-permute-start | bytes 196616 | tf_op jit(solution)/shard_map/ppermute | solution.py:25
  100.4 7.4 %all-to-all-done.1.rest_0_ = bf16[8,64,512]{2,1,0:T(8,128)(2,1)} async-done(((bf16[8,64,512]{2,1,0:T(8,128)(2,1)}), bf16[8,64,512]{2,1,0:T(8,128)(2,1)}, u32[]{:S(2)}, u32[]{:S(2)}) %all-to-all-start.1) | async-done | bytes 524320 | tf_op jit(solution)/shard_map/all_to_all | solution.py:230
  107.9 6.9 %all-to-all-start.2 = ((bf16[32,16,512]{2,1,0:T(8,128)(2,1)}), bf16[32,16,512]{2,1,0:T(8,128)(2,1)}, u32[]{:S(2)}, u32[]{:S(2)}) async-start(bf16[32,16,512]{2,1,0:T(8,128)(2,1)} %bitcast.131), calls=%async_computation.2 | async-start | bytes 1048576 | tf_op jit(solution)/shard_map/all_to_all | solution.py:287
  120.6 10.2 %collective-permute-done.29.rest_11_ = bf16[4,64,512]{2,1,0:T(8,128)(2,1)S(1)} collective-permute-done((bf16[4,64,512]{2,1,0:T(8,128)(2,1)S(1)}, bf16[4,64,512]{2,1,0:T(8,128)(2,1)S(1)}, u32[]{:S(2)}, u32[]{:S(2)}) %collective-permute-start.29) | collective-permute-done | bytes 262176 | tf_op jit(solution)/shard_map/ppermute | solution.py:21
  131.5 3.2 %collective-permute-start.27 = (bf16[4,64,512]{2,1,0:T(8,128)(2,1)S(1)}, bf16[4,64,512]{2,1,0:T(8,128)(2,1)}, u32[]{:S(2)}, u32[]{:S(2)}) collective-permute-start(bf16[4,64,512]{2,1,0:T(8,128)(2,1)S(1)} %collective-permute-done.26.rest_5_), channel_id=1, source_target_pairs={{0,28},{1,29},{2,30},{3,31},{4,0},{5,1},{6,2},{7,3},{8,4},{9,5},{1... | collective-permute-start | bytes 786440 | tf_op jit(solution)/shard_map/ppermute | solution.py:21
  135.4 5.6 %collective-permute-done.30.rest_10_ = bf16[4,64,512]{2,1,0:T(8,128)(2,1)S(1)} collective-permute-done((bf16[4,64,512]{2,1,0:T(8,128)(2,1)S(1)}, bf16[4,64,512]{2,1,0:T(8,128)(2,1)S(1)}, u32[]{:S(2)}, u32[]{:S(2)}) %collective-permute-start.30) | collective-permute-done | bytes 262176 | tf_op jit(solution)/shard_map/ppermute | solution.py:21
  143.8 3.2 %collective-permute-start.28 = (bf16[4,64,512]{2,1,0:T(8,128)(2,1)}, bf16[4,64,512]{2,1,0:T(8,128)(2,1)}, u32[]{:S(2)}, u32[]{:S(2)}) collective-permute-start(bf16[4,64,512]{2,1,0:T(8,128)(2,1)} %collective-permute-done.27.rest_6_), channel_id=1, source_target_pairs={{0,28},{1,29},{2,30},{3,31},{4,0},{5,1},{6,2},{7,3},{8,4},{9,5},{1... | collective-permute-start | bytes 786440 | tf_op jit(solution)/shard_map/ppermute | solution.py:21
  147.0 3.9 %collective-permute-done.31.rest_9_ = bf16[4,64,512]{2,1,0:T(8,128)(2,1)} collective-permute-done((bf16[4,64,512]{2,1,0:T(8,128)(2,1)S(1)}, bf16[4,64,512]{2,1,0:T(8,128)(2,1)}, u32[]{:S(2)}, u32[]{:S(2)}) %collective-permute-start.31) | collective-permute-done | bytes 262176 | tf_op jit(solution)/shard_map/ppermute | solution.py:21
  163.5 8.8 %backward_blocks.1 = (f32[512,512]{1,0:T(8,128)S(1)}, bf16[512,512]{1,0:T(8,128)(2,1)S(1)}) custom-call(s32[256]{0:T(256)S(1)} %select_reduce_fusion.table, s32[2]{0:T(128)S(1)} %pad_add_fusion.place, bf16[96,128,128]{2,1,0:T(8,128)(2,1)S(1)} %copy-done.3, bf16[8,64,512]{2,1,0:T(8,128)(2,1)} %all-to-all-done.1.rest_0_, ...), custom_call_target="tpu_custom_call" | custom-call | tf_op jit(solution)/shard_map/backward_blocks/pallas_call | solution.py:195
  181.7 2.8 %collective-permute-done.38 = bf16[144,512]{1,0:T(8,128)(2,1)S(1)} collective-permute-done((bf16[144,512]{1,0:T(8,128)(2,1)S(1)}, bf16[144,512]{1,0:T(8,128)(2,1)S(1)}, u32[]{:S(2)}, u32[]{:S(2)}) %collective-permute-start.38) | collective-permute-done | bytes 147488 | tf_op jit(solution)/shard_map/ppermute | solution.py:29
  (155 shorter events, 77.0 us)
Async XLA Ops:
  24.9 9.0 %collective-permute-start.8 = (bf16[2,48,512]{2,1,0:T(8,128)(2,1)S(1)}, bf16[2,48,512]{2,1,0:T(8,128)(2,1)S(1)}, u32[]{:S(2)}, u32[]{:S(2)}) collective-permute-start(bf16[2,48,512]{2,1,0:T(8,128)(2,1)S(1)} %get-tuple-element.25), channel_id=1, source_target_pairs={{0,4},{1,5},{2,6},{3,7},{4,8},{5,9},{6,10},{7,11},{8,12},{9,13},{1... | collective-permute-start | bytes 294920 | tf_op jit(solution)/shard_map/ppermute | solution.py:21
  34.0 7.7 %collective-permute-start.9 = (bf16[4,48,512]{2,1,0:T(8,128)(2,1)S(1)}, bf16[4,48,512]{2,1,0:T(8,128)(2,1)S(1)}, u32[]{:S(2)}, u32[]{:S(2)}) collective-permute-start(bf16[4,48,512]{2,1,0:T(8,128)(2,1)S(1)} %pad_maximum_fusion.5), channel_id=1, source_target_pairs={{0,4},{1,5},{2,6},{3,7},{4,8},{5,9},{6,10},{7,11},{8,12},{9,13},{1... | collective-permute-start | bytes 589832 | tf_op jit(solution)/shard_map/ppermute | solution.py:21
  34.1 9.3 %collective-permute-start.6 = (bf16[4,80,512]{2,1,0:T(8,128)(2,1)S(1)}, bf16[4,80,512]{2,1,0:T(8,128)(2,1)S(1)}, u32[]{:S(2)}, u32[]{:S(2)}) collective-permute-start(bf16[4,80,512]{2,1,0:T(8,128)(2,1)S(1)} %get-tuple-element.30), channel_id=1, source_target_pairs={{0,3},{1,0},{2,1},{3,2},{4,7},{5,4},{6,5},{7,6},{8,11},{9,8},{10,9... | collective-permute-start | bytes 983048 | tf_op jit(solution)/shard_map/ppermute | solution.py:25
  34.7 10.2 %collective-permute-start.4 = (bf16[4,80,512]{2,1,0:T(8,128)(2,1)S(1)}, bf16[4,80,512]{2,1,0:T(8,128)(2,1)S(1)}, u32[]{:S(2)}, u32[]{:S(2)}) collective-permute-start(bf16[4,80,512]{2,1,0:T(8,128)(2,1)S(1)} %get-tuple-element.29), channel_id=1, source_target_pairs={{0,1},{1,2},{2,3},{3,0},{4,5},{5,6},{6,7},{7,4},{8,9},{9,10},{10,1... | collective-permute-start | bytes 983048 | tf_op jit(solution)/shard_map/ppermute | solution.py:25
  36.4 9.5 %collective-permute-start.13 = (bf16[4,48,512]{2,1,0:T(8,128)(2,1)S(1)}, bf16[4,48,512]{2,1,0:T(8,128)(2,1)S(1)}, u32[]{:S(2)}, u32[]{:S(2)}) collective-permute-start(bf16[4,48,512]{2,1,0:T(8,128)(2,1)S(1)} %pad_maximum_fusion.6), channel_id=1, source_target_pairs={{0,28},{1,29},{2,30},{3,31},{4,0},{5,1},{6,2},{7,3},{8,4},{9,5},{1... | collective-permute-start | bytes 589832 | tf_op jit(solution)/shard_map/ppermute | solution.py:21
  43.5 15.4 %collective-permute-start.7 = (bf16[8,80,512]{2,1,0:T(8,128)(2,1)S(1)}, bf16[8,80,512]{2,1,0:T(8,128)(2,1)S(1)}, u32[]{:S(2)}, u32[]{:S(2)}) collective-permute-start(bf16[8,80,512]{2,1,0:T(8,128)(2,1)S(1)} %pad_maximum_fusion.1), channel_id=1, source_target_pairs={{0,3},{1,0},{2,1},{3,2},{4,7},{5,4},{6,5},{7,6},{8,11},{9,8},{10,9... | collective-permute-start | bytes 1966088 | tf_op jit(solution)/shard_map/ppermute | solution.py:25
  45.1 16.7 %collective-permute-start.5 = (bf16[8,80,512]{2,1,0:T(8,128)(2,1)S(1)}, bf16[8,80,512]{2,1,0:T(8,128)(2,1)S(1)}, u32[]{:S(2)}, u32[]{:S(2)}) collective-permute-start(bf16[8,80,512]{2,1,0:T(8,128)(2,1)S(1)} %pad_maximum_fusion), channel_id=1, source_target_pairs={{0,1},{1,2},{2,3},{3,0},{4,5},{5,6},{6,7},{7,4},{8,9},{9,10},{10,1... | collective-permute-start | bytes 1966088 | tf_op jit(solution)/shard_map/ppermute | solution.py:25
  49.2 18.8 %collective-permute-start.11 = (bf16[4,48,512]{2,1,0:T(8,128)(2,1)S(1)}, bf16[4,48,512]{2,1,0:T(8,128)(2,1)S(1)}, u32[]{:S(2)}, u32[]{:S(2)}) collective-permute-start(bf16[4,48,512]{2,1,0:T(8,128)(2,1)S(1)} %get-tuple-element.21), channel_id=1, source_target_pairs={{0,4},{1,5},{2,6},{3,7},{4,8},{5,9},{6,10},{7,11},{8,12},{9,13},{1... | collective-permute-start | bytes 589832 | tf_op jit(solution)/shard_map/ppermute | solution.py:21
  55.1 12.8 %collective-permute-start.15 = (bf16[4,48,512]{2,1,0:T(8,128)(2,1)S(1)}, bf16[4,48,512]{2,1,0:T(8,128)(2,1)S(1)}, u32[]{:S(2)}, u32[]{:S(2)}) collective-permute-start(bf16[4,48,512]{2,1,0:T(8,128)(2,1)S(1)} %fusion.2), channel_id=1, source_target_pairs={{0,28},{1,29},{2,30},{3,31},{4,0},{5,1},{6,2},{7,3},{8,4},{9,5},{1... | collective-permute-start | bytes 589832 | tf_op jit(solution)/shard_map/ppermute | solution.py:21
  63.0 22.8 %all-to-all-start = ((bf16[8,80,512]{2,1,0:T(8,128)(2,1)}), bf16[8,80,512]{2,1,0:T(8,128)(2,1)S(1)}, u32[]{:S(2)}, u32[]{:S(2)}) async-start(bf16[8,80,512]{2,1,0:T(8,128)(2,1)} %add_convert_fusion), calls=%async_computation | async-start | bytes 1310720 | tf_op jit(solution)/shard_map/all_to_all | solution.py:230
  88.7 19.2 %all-to-all-start.1 = ((bf16[8,64,512]{2,1,0:T(8,128)(2,1)}), bf16[8,64,512]{2,1,0:T(8,128)(2,1)}, u32[]{:S(2)}, u32[]{:S(2)}) async-start(bf16[8,64,512]{2,1,0:T(8,128)(2,1)} %broadcast_in_dim.17), calls=%async_computation.1 | async-start | bytes 1048576 | tf_op jit(solution)/shard_map/all_to_all | solution.py:230
  93.5 21.3 %collective-permute-start.23 = (bf16[64,512]{1,0:T(8,128)(2,1)}, bf16[64,512]{1,0:T(8,128)(2,1)}, u32[]{:S(2)}, u32[]{:S(2)}) collective-permute-start(bf16[64,512]{1,0:T(8,128)(2,1)} %get-tuple-element.44), channel_id=1, source_target_pairs={{0,3},{1,0},{2,1},{3,2},{4,7},{5,4},{6,5},{7,6},{8,11},{9,8},{10,9... | collective-permute-start | bytes 196616 | tf_op jit(solution)/shard_map/ppermute | solution.py:25
  99.3 15.5 %collective-permute-start.25 = (bf16[64,512]{1,0:T(8,128)(2,1)}, bf16[64,512]{1,0:T(8,128)(2,1)}, u32[]{:S(2)}, u32[]{:S(2)}) collective-permute-start(bf16[64,512]{1,0:T(8,128)(2,1)} %collective-permute-done.24), channel_id=1, source_target_pairs={{0,1},{1,2},{2,3},{3,0},{4,5},{5,6},{6,7},{7,4},{8,9},{9,10},{10,1... | collective-permute-start | bytes 196616 | tf_op jit(solution)/shard_map/ppermute | solution.py:25
  107.9 47.5 %all-to-all-start.2 = ((bf16[32,16,512]{2,1,0:T(8,128)(2,1)}), bf16[32,16,512]{2,1,0:T(8,128)(2,1)}, u32[]{:S(2)}, u32[]{:S(2)}) async-start(bf16[32,16,512]{2,1,0:T(8,128)(2,1)} %bitcast.131), calls=%async_computation.2 | async-start | bytes 1048576 | tf_op jit(solution)/shard_map/all_to_all | solution.py:287
  115.8 15.0 %collective-permute-start.29 = (bf16[4,64,512]{2,1,0:T(8,128)(2,1)S(1)}, bf16[4,64,512]{2,1,0:T(8,128)(2,1)S(1)}, u32[]{:S(2)}, u32[]{:S(2)}) collective-permute-start(bf16[4,64,512]{2,1,0:T(8,128)(2,1)S(1)} %pad_maximum_fusion.4.rest_4_), channel_id=1, source_target_pairs={{0,4},{1,5},{2,6},{3,7},{4,8},{5,9},{6,10},{7,11},{8,12},{9,13},{1... | collective-permute-start | bytes 786440 | tf_op jit(solution)/shard_map/ppermute | solution.py:21
  117.4 24.8 %collective-permute-start.21 = (bf16[8,64,512]{2,1,0:T(8,128)(2,1)}, bf16[8,64,512]{2,1,0:T(8,128)(2,1)}, u32[]{:S(2)}, u32[]{:S(2)}) collective-permute-start(bf16[8,64,512]{2,1,0:T(8,128)(2,1)} %all-to-all-done.1.rest_0_), channel_id=1, source_target_pairs={{0,1},{1,2},{2,3},{3,0},{4,5},{5,6},{6,7},{7,4},{8,9},{9,10},{10,1... | collective-permute-start | bytes 1572872 | tf_op jit(solution)/shard_map/ppermute | solution.py:25
  118.8 12.7 %collective-permute-start.26 = (bf16[4,64,512]{2,1,0:T(8,128)(2,1)S(1)}, bf16[4,64,512]{2,1,0:T(8,128)(2,1)S(1)}, u32[]{:S(2)}, u32[]{:S(2)}) collective-permute-start(bf16[4,64,512]{2,1,0:T(8,128)(2,1)S(1)} %pad_maximum_fusion.4.rest_4_), channel_id=1, source_target_pairs={{0,28},{1,29},{2,30},{3,31},{4,0},{5,1},{6,2},{7,3},{8,4},{9,5},{1... | collective-permute-start | bytes 786440 | tf_op jit(solution)/shard_map/ppermute | solution.py:21
  130.8 10.3 %collective-permute-start.30 = (bf16[4,64,512]{2,1,0:T(8,128)(2,1)S(1)}, bf16[4,64,512]{2,1,0:T(8,128)(2,1)S(1)}, u32[]{:S(2)}, u32[]{:S(2)}) collective-permute-start(bf16[4,64,512]{2,1,0:T(8,128)(2,1)S(1)} %collective-permute-done.29.rest_11_), channel_id=1, source_target_pairs={{0,4},{1,5},{2,6},{3,7},{4,8},{5,9},{6,10},{7,11},{8,12},{9,13},{1... | collective-permute-start | bytes 786440 | tf_op jit(solution)/shard_map/ppermute | solution.py:21
  131.5 12.3 %collective-permute-start.27 = (bf16[4,64,512]{2,1,0:T(8,128)(2,1)S(1)}, bf16[4,64,512]{2,1,0:T(8,128)(2,1)}, u32[]{:S(2)}, u32[]{:S(2)}) collective-permute-start(bf16[4,64,512]{2,1,0:T(8,128)(2,1)S(1)} %collective-permute-done.26.rest_5_), channel_id=1, source_target_pairs={{0,28},{1,29},{2,30},{3,31},{4,0},{5,1},{6,2},{7,3},{8,4},{9,5},{1... | collective-permute-start | bytes 786440 | tf_op jit(solution)/shard_map/ppermute | solution.py:21
  141.0 9.9 %collective-permute-start.31 = (bf16[4,64,512]{2,1,0:T(8,128)(2,1)S(1)}, bf16[4,64,512]{2,1,0:T(8,128)(2,1)}, u32[]{:S(2)}, u32[]{:S(2)}) collective-permute-start(bf16[4,64,512]{2,1,0:T(8,128)(2,1)S(1)} %collective-permute-done.30.rest_10_), channel_id=1, source_target_pairs={{0,4},{1,5},{2,6},{3,7},{4,8},{5,9},{6,10},{7,11},{8,12},{9,13},{1... | collective-permute-start | bytes 786440 | tf_op jit(solution)/shard_map/ppermute | solution.py:21
  141.7 17.0 %collective-permute-start.20 = (bf16[8,64,512]{2,1,0:T(8,128)(2,1)}, bf16[8,64,512]{2,1,0:T(8,128)(2,1)}, u32[]{:S(2)}, u32[]{:S(2)}) collective-permute-start(bf16[8,64,512]{2,1,0:T(8,128)(2,1)} %all-to-all-done.1.rest_0_), channel_id=1, source_target_pairs={{0,3},{1,0},{2,1},{3,2},{4,7},{5,4},{6,5},{7,6},{8,11},{9,8},{10,9... | collective-permute-start | bytes 1572872 | tf_op jit(solution)/shard_map/ppermute | solution.py:25
  142.2 16.6 %collective-permute-start.22 = (bf16[8,64,512]{2,1,0:T(8,128)(2,1)}, bf16[8,64,512]{2,1,0:T(8,128)(2,1)}, u32[]{:S(2)}, u32[]{:S(2)}) collective-permute-start(bf16[8,64,512]{2,1,0:T(8,128)(2,1)} %collective-permute-done.21.rest_3_), channel_id=1, source_target_pairs={{0,1},{1,2},{2,3},{3,0},{4,5},{5,6},{6,7},{7,4},{8,9},{9,10},{10,1... | collective-permute-start | bytes 1572872 | tf_op jit(solution)/shard_map/ppermute | solution.py:25
  143.8 12.9 %collective-permute-start.28 = (bf16[4,64,512]{2,1,0:T(8,128)(2,1)}, bf16[4,64,512]{2,1,0:T(8,128)(2,1)}, u32[]{:S(2)}, u32[]{:S(2)}) collective-permute-start(bf16[4,64,512]{2,1,0:T(8,128)(2,1)} %collective-permute-done.27.rest_6_), channel_id=1, source_target_pairs={{0,28},{1,29},{2,30},{3,31},{4,0},{5,1},{6,2},{7,3},{8,4},{9,5},{1... | collective-permute-start | bytes 786440 | tf_op jit(solution)/shard_map/ppermute | solution.py:21
  150.9 7.9 %collective-permute-start.32 = (bf16[4,64,512]{2,1,0:T(8,128)(2,1)}, bf16[4,64,512]{2,1,0:T(8,128)(2,1)}, u32[]{:S(2)}, u32[]{:S(2)}) collective-permute-start(bf16[4,64,512]{2,1,0:T(8,128)(2,1)} %collective-permute-done.31.rest_9_), channel_id=1, source_target_pairs={{0,4},{1,5},{2,6},{3,7},{4,8},{5,9},{6,10},{7,11},{8,12},{9,13},{1... | collective-permute-start | bytes 786440 | tf_op jit(solution)/shard_map/ppermute | solution.py:21
  (34 other events, 260.5 us)
where the time goes:
time: 190 us; the launch traced here: 189 us
  waiting for transfers between devices  82.2 us (43%)
  starting transfers between devices  64.8 us (34%)
  Pallas kernels  16.6 us (9%)
  local copies, waits for them, and re-layouts  14.5 us (8%)
  other arithmetic  5.95 us (3%)
  matrix products  3.74 us (2%)
    ppermute x15, waiting for transfers between devices, shift(): lax.ppermute(value, 'col', [(i, (i // NY + step) % NZ * NY + i % NY) for...  33.7 us
    ppermute x15, starting transfers between devices, shift(): lax.ppermute(value, 'col', [(i, (i // NY + step) % NZ * NY + i % NY) for...  22.4 us
    ppermute x14, waiting for transfers between devices, shift(): lax.ppermute(value, 'col', [(i, i // NY * NY + (i % NY + step) % NY) for...  18.6 us
    ppermute x14, starting transfers between devices, shift(): lax.ppermute(value, 'col', [(i, i // NY * NY + (i % NY + step) % NY) for...  17.2 us
    ppermute x7, waiting for transfers between devices, shift(): lax.ppermute(value, 'row', [(i, (i // NC + step) % NX * NC + i % NC) for...  16.8 us
    unnamed x33, local copies, waits for them, and re-layouts  11.8 us
    all_to_all x2, waiting for transfers between devices, exchange(): lax.all_to_all(parts, 'col', 0, 0, axis_index_groups=groups, tiled=True)  10.2 us
    all_to_all x2, starting transfers between devices, exchange(): lax.all_to_all(parts, 'col', 0, 0, axis_index_groups=groups, tiled=True)  9.46 us
  transfers between devices with their start and end apart: 42, of which 27 were waited for; matrix products, arithmetic and copies ran while one was open for 3% of the time, Pallas kernels for 1%

commit v1 on v0

--- a/solution.py
+++ b/solution.py
@@ -9,8 +9,7 @@
 BLK = 128
 NB = 96
 NX, NC, NZ, NY = 4, 2, 8, 4
-HALF = BLK // 2
-TOP = 80
+TOP = 96
 PIECES = 2
 F32 = jnp.float32
 BF16 = jnp.bfloat16
@@ -56,15 +55,20 @@
     return own + right + left
 
 
-def ring_gather(own, axis, count):
+def ring_gather(own, axis, count, halves=False):
+    far = count // 2
+    cut = own.shape[0] // 2
     pieces = [None] * count
     pieces[0] = right = left = own
-    for step in range(1, count // 2 + 1):
-        right = shift(right, axis, 1)
+    for step in range(1, far + 1):
+        last = halves and step == far
+        right = shift(right[:cut] if last else right, axis, 1)
         pieces[count - step] = right
-        if step < count - step:
-            left = shift(left, axis, -1)
+        if step < far or last:
+            left = shift(left[cut:] if last else left, axis, -1)
             pieces[step] = left
+    if halves:
+        pieces[far : far + 1] = [right, left]
     return pieces
 
 
@@ -121,7 +125,9 @@
             grid=(NZ,),
             in_specs=[whole(NB, BLK, BLK)] + [pl.BlockSpec(memory_space=pltpu.HBM)] * len(pieces),
             out_specs=[yspec] * NY
-            + [pl.BlockSpec((1, NY, BLK - TOP, HID), lambda g, t, p: (g, 0, 0, 0))],
+            + [pl.BlockSpec(
+                (1, NY, BLK - TOP, HID), lambda g, t, p: (lax.rem(g + p[0], NZ), 0, 0, 0)
+            )],
             scratch_shapes=[
                 pltpu.VMEM((nodes, HID), BF16),
                 pltpu.VMEM((NY * BLK, nodes), BF16),
@@ -155,17 +161,24 @@
     )(after, vals)
 
 
-def backward_kernel(table, place, vals, *rest):
-    pieces = rest[: NY + NZ]
-    near, away, slope, acc, lhs, sems = rest[NY + NZ :]
+def backward_kernel(table, vals, *rest):
+    pieces = rest[: NY + 2]
+    near, away, slope, acc, lhs, sems = rest[NY + 2 :]
     turn = pl.program_id(0)
 
     @pl.when(turn == 0)
     def _():
-        lower, upper = pl.ds(0, HALF), pl.ds(HALF, HALF)
-        moves = [(pieces[k], slope.at[:, k, lower]) for k in range(NY)]
-        for k in range(NZ):
-            moves.append((pieces[NY + k], slope.at[lax.rem(place[0] + k, NZ), :, upper]))
+        lower, upper = pl.ds(0, TOP), pl.ds(TOP, BLK - TOP)
+        cut = NZ // 2
+        y0, y1, y2a, y2b, y3, others = pieces
+        moves = [
+            (y0, slope.at[:, 0, lower]),
+            (y1, slope.at[:, 1, lower]),
+            (y2a, slope.at[pl.ds(0, cut), 2, lower]),
+            (y2b, slope.at[pl.ds(cut, cut), 2, lower]),
+            (y3, slope.at[:, 3, lower]),
+            (others, slope.at[:, :, upper]),
+        ]
         copies = [
             pltpu.make_async_copy(src, dst, sems.at[k]) for k, (src, dst) in enumerate(moves)
         ]
@@ -190,12 +203,12 @@
         away[...] = acc[NX * BLK :].astype(BF16)
 
 
-def backward_blocks(table, place, vals, pieces):
+def backward_blocks(table, vals, pieces):
     nodes = NX * NC * BLK
     return pl.pallas_call(
         backward_kernel,
         grid_spec=pltpu.PrefetchScalarGridSpec(
-            num_scalar_prefetch=2,
+            num_scalar_prefetch=1,
             grid=(NZ,),
             in_specs=[whole(NB, BLK, BLK)] + [pl.BlockSpec(memory_space=pltpu.HBM)] * len(pieces),
             out_specs=[whole(NX * BLK, HID), whole(NX * BLK, HID)],
@@ -212,7 +225,7 @@
         ],
         compiler_params=pltpu.CompilerParams(vmem_limit_bytes=20 << 20),
         name="backward_blocks",
-    )(table, place, vals, *pieces)
+    )(table, vals, *pieces)
 
 
 def slot_table(block_rows, block_cols, live):
@@ -257,7 +270,8 @@
     y0, y1, y2, y3, zo = forward_blocks(forward_table, place, values, gathered)
     values_t = turned(values, zo)
     by_y = ring_sum([y0, y1, y2, y3], "y").astype(BF16)
-    by_z = ring_sum([zo[k] for k in range(NZ)], "z")
+    by_z = exchange(zo, ZGROUPS)
+    by_z = jnp.sum(by_z.astype(F32), axis=0)
     top = exchange(by_y, ZGROUPS)
     bottom = ring_sum([by_z[k] for k in range(NY)], "y", wire=F32)
     top = jnp.sum(top.astype(F32), axis=0)
@@ -273,11 +287,10 @@
     slope = cotangent.astype(F32) * sigma * (1.0 + total * (1.0 - sigma))
     slope = slope.astype(BF16)
 
-    top_all = spread(slope[:HALF], ZGROUPS)
-    bottom_all = jnp.stack(ring_gather(slope[HALF:], "y", NY))
-    ypieces = ring_gather(top_all, "y", NY)
-    zpieces = ring_gather(bottom_all, "z", NZ)
-    pieces = ypieces + zpieces
+    top_all = spread(slope[:TOP], ZGROUPS)
+    bottom_all = jnp.stack(ring_gather(slope[TOP:], "y", NY))
+    ypieces = ring_gather(top_all, "y", NY, halves=True)
+    pieces = ypieces + [spread(bottom_all, ZGROUPS)]
 
     part, width = HID // (NX * NC), HID // (NZ * NY)
     pull = lambda left: lax.dot_general(
@@ -292,7 +305,7 @@
     other = lax.dynamic_index_in_dim(shares, 1 - core, 1, keepdims=False)
     mine = mine + shift(other, "core", 1)
 
-    near, away = backward_blocks(backward_table, place, values_t, pieces)
+    near, away = backward_blocks(backward_table, values_t, pieces)
     near = near + shift(away, "core", 1).astype(F32)
     spare = jnp.zeros((NX, 16 - mine.shape[1], HID), F32)
     both = jnp.concatenate([near.reshape(NX, BLK, HID), mine, spare], 1)

time: 190 us -> 212 us (1.12)
  the two profiles are of different devices: /device:TPU:8 before, /device:TPU:24 now
where the time goes in v1:
time: 212 us; the launch traced here: 211 us
  waiting for transfers between devices  109 us (51%)
  starting transfers between devices  57.5 us (27%)
  local copies, waits for them, and re-layouts  16.8 us (8%)
  Pallas kernels  16.7 us (8%)
  other arithmetic  5.88 us (3%)
  matrix products  3.74 us (2%)
    ppermute x15, waiting for transfers between devices, shift(): lax.ppermute(value, 'col', [(i, i // NY * NY + (i % NY + step) % NY) for...  47.5 us
    all_to_all x4, waiting for transfers between devices, exchange(): lax.all_to_all(parts, 'col', 0, 0, axis_index_groups=groups, tiled=True)  25.6 us
    ppermute x15, starting transfers between devices, shift(): lax.ppermute(value, 'col', [(i, i // NY * NY + (i % NY + step) % NY) for...  22.7 us
    all_to_all x4, starting transfers between devices, exchange(): lax.all_to_all(parts, 'col', 0, 0, axis_index_groups=groups, tiled=True)  20.4 us
    ppermute x7, waiting for transfers between devices, shift(): lax.ppermute(value, 'row', [(i, (i // NC + step) % NX * NC + i % NC) for...  17.2 us
    all_to_all x1, waiting for transfers between devices, on_device(): shares = lax.all_to_all(local, 'col', 0, 0, tiled=True)  16.1 us
    unnamed x35, local copies, waits for them, and re-layouts  10.4 us
    pallas_call x1, Pallas kernels, backward_blocks(): pl.pallas_call(backward_kernel, grid_spec=pltpu.PrefetchScalarGridSpec(nu...  8.15 us
  transfers between devices with their start and end apart: 30, of which 23 were waited for; matrix products, arithmetic and copies ran while one was open for 3% of the time, Pallas kernels for 1%

profile of v1, /device:TPU:24, one launch (start us, length us, event | category | flops | bytes accessed | tf_op | source)
XLA Modules:
  0.0 211.1 jit_solution(8639603093078719068)
XLA Ops:
  4.9 3.2 %collective-permute-done.1 = bf16[128,512]{1,0:T(8,128)(2,1)S(1)} collective-permute-done((bf16[128,512]{1,0:T(8,128)(2,1)S(1)}, bf16[128,512]{1,0:T(8,128)(2,1)S(1)}, u32[]{:S(2)}, u32[]{:S(2)}) %collective-permute-start.1) | collective-permute-done | bytes 131104 | tf_op jit(solution)/shard_map/ppermute | solution.py:28
  8.5 5.8 %collective-permute-done.2 = bf16[128,512]{1,0:T(8,128)(2,1)S(1)} collective-permute-done((bf16[128,512]{1,0:T(8,128)(2,1)S(1)}, bf16[128,512]{1,0:T(8,128)(2,1)S(1)}, u32[]{:S(2)}, u32[]{:S(2)}) %collective-permute-start.2) | collective-permute-done | bytes 131104 | tf_op jit(solution)/shard_map/ppermute | solution.py:28
  18.2 7.3 %forward_blocks.1 = (bf16[8,96,512]{2,1,0:T(8,128)(2,1)S(1)}, bf16[8,96,512]{2,1,0:T(8,128)(2,1)S(1)}, bf16[8,96,512]{2,1,0:T(8,128)(2,1)S(1)}, bf16[8,96,512]{2,1,0:T(8,128)(2,1)S(1)}, bf16[8,4,32,512]{3,2,1,0:T(8,128)(2,1)}) custom-call(s32[256]{0:T(256)S(1)} %select_reduce_fusion.1.table, s32[2]{0:T(128)S(1)} %pad_add_fusion.place, ...), custom_call_target="tpu_custom_call" | custom-call | tf_op jit(solution)/shard_map/forward_blocks/pallas_call | solution.py:121
  27.2 2.5 %collective-permute-start.4 = (bf16[4,96,512]{2,1,0:T(8,128)(2,1)}, bf16[4,96,512]{2,1,0:T(8,128)(2,1)}, u32[]{:S(2)}, u32[]{:S(2)}) collective-permute-start(bf16[4,96,512]{2,1,0:T(8,128)(2,1)} %get-tuple-element.21), channel_id=1, source_target_pairs={{0,1},{1,2},{2,3},{3,0},{4,5},{5,6},{6,7},{7,4},{8,9},{9,10},{10,1... | collective-permute-start | bytes 1179656 | tf_op jit(solution)/shard_map/ppermute | solution.py:24
  29.7 8.5 %all-to-all-start.1 = ((bf16[8,4,32,512]{3,2,1,0:T(8,128)(2,1)}), bf16[8,4,32,512]{3,2,1,0:T(8,128)(2,1)S(1)}, u32[]{:S(2)}, u32[]{:S(2)}) async-start(bf16[8,4,32,512]{3,2,1,0:T(8,128)(2,1)} %get-tuple-element.14.after), calls=%async_computation.1 | async-start | bytes 2097152 | tf_op jit(solution)/shard_map/all_to_all | solution.py:243
  41.6 3.3 %collective-permute-start.5 = (bf16[8,96,512]{2,1,0:T(8,128)(2,1)S(1)}, bf16[8,96,512]{2,1,0:T(8,128)(2,1)S(1)}, u32[]{:S(2)}, u32[]{:S(2)}) collective-permute-start(bf16[8,96,512]{2,1,0:T(8,128)(2,1)S(1)} %pad_maximum_fusion), channel_id=1, source_target_pairs={{0,1},{1,2},{2,3},{3,0},{4,5},{5,6},{6,7},{7,4},{8,9},{9,10},{10,1... | collective-permute-start | bytes 2359304 | tf_op jit(solution)/shard_map/ppermute | solution.py:24
  44.9 15.4 %collective-permute-done.7 = bf16[8,96,512]{2,1,0:T(8,128)(2,1)S(1)} collective-permute-done((bf16[8,96,512]{2,1,0:T(8,128)(2,1)S(1)}, bf16[8,96,512]{2,1,0:T(8,128)(2,1)S(1)}, u32[]{:S(2)}, u32[]{:S(2)}) %collective-permute-start.7) | collective-permute-done | bytes 786464 | tf_op jit(solution)/shard_map/ppermute | solution.py:24
  62.1 4.6 %all-to-all-done.1 = bf16[8,4,32,512]{3,2,1,0:T(8,128)(2,1)S(1)} async-done(((bf16[8,4,32,512]{3,2,1,0:T(8,128)(2,1)}), bf16[8,4,32,512]{3,2,1,0:T(8,128)(2,1)S(1)}, u32[]{:S(2)}, u32[]{:S(2)}) %all-to-all-start.1) | async-done | bytes 1048608 | tf_op jit(solution)/shard_map/all_to_all | solution.py:243
  66.6 3.9 %all-to-all-start = ((bf16[8,96,512]{2,1,0:T(8,128)(2,1)}), bf16[8,96,512]{2,1,0:T(8,128)(2,1)S(1)}, u32[]{:S(2)}, u32[]{:S(2)}) async-start(bf16[8,96,512]{2,1,0:T(8,128)(2,1)} %add_convert_fusion), calls=%async_computation | async-start | bytes 1572864 | tf_op jit(solution)/shard_map/all_to_all | solution.py:243
  70.7 3.8 %collective-permute-start.8 = (f32[16,512]{1,0:T(8,128)S(1)}, f32[16,512]{1,0:T(8,128)S(1)}, u32[]{:S(2)}, u32[]{:S(2)}) collective-permute-start(f32[16,512]{1,0:T(8,128)S(1)} %get-tuple-element.31), channel_id=1, source_target_pairs={{0,1},{1,2},{2,3},{3,0},{4,5},{5,6},{6,7},{7,4},{8,9},{9,10},{10,1... | collective-permute-start | bytes 98312 | tf_op jit(solution)/shard_map/ppermute | solution.py:24
  76.1 3.5 %collective-permute-done.10 = f32[16,512]{1,0:T(8,128)S(1)} collective-permute-done((f32[16,512]{1,0:T(8,128)S(1)}, f32[16,512]{1,0:T(8,128)S(1)}, u32[]{:S(2)}, u32[]{:S(2)}) %collective-permute-start.10) | collective-permute-done | bytes 32800 | tf_op jit(solution)/shard_map/ppermute | solution.py:24
  79.7 3.2 %collective-permute-start.9 = (f32[32,512]{1,0:T(8,128)S(1)}, f32[32,512]{1,0:T(8,128)S(1)}, u32[]{:S(2)}, u32[]{:S(2)}) collective-permute-start(f32[32,512]{1,0:T(8,128)S(1)} %pad_maximum_fusion.7), channel_id=1, source_target_pairs={{0,1},{1,2},{2,3},{3,0},{4,5},{5,6},{6,7},{7,4},{8,9},{9,10},{10,1... | collective-permute-start | bytes 196616 | tf_op jit(solution)/shard_map/ppermute | solution.py:24
  85.2 8.4 %all-to-all-done = bf16[8,96,512]{2,1,0:T(8,128)(2,1)S(1)} async-done(((bf16[8,96,512]{2,1,0:T(8,128)(2,1)}), bf16[8,96,512]{2,1,0:T(8,128)(2,1)S(1)}, u32[]{:S(2)}, u32[]{:S(2)}) %all-to-all-start) | async-done | bytes 786464 | tf_op jit(solution)/shard_map/all_to_all | solution.py:243
  96.5 5.7 %all-to-all-start.4 = ((bf16[32,16,512]{2,1,0:T(8,128)(2,1)}), bf16[32,16,512]{2,1,0:T(8,128)(2,1)S(1)}, u32[]{:S(2)}, u32[]{:S(2)}) async-start(bf16[32,16,512]{2,1,0:T(8,128)(2,1)} %bitcast.17), calls=%async_computation.4 | async-start | bytes 1048576 | tf_op jit(solution)/shard_map/all_to_all | solution.py:300
  102.3 16.1 %all-to-all-done.4 = bf16[32,16,512]{2,1,0:T(8,128)(2,1)S(1)} async-done(((bf16[32,16,512]{2,1,0:T(8,128)(2,1)}), bf16[32,16,512]{2,1,0:T(8,128)(2,1)S(1)}, u32[]{:S(2)}, u32[]{:S(2)}) %all-to-all-start.4) | async-done | bytes 524320 | tf_op jit(solution)/shard_map/all_to_all | solution.py:300
  119.4 3.5 %all-to-all-start.2 = ((bf16[8,96,512]{2,1,0:T(8,128)(2,1)}), bf16[8,96,512]{2,1,0:T(8,128)(2,1)S(1)}, u32[]{:S(2)}, u32[]{:S(2)}) async-start(bf16[8,96,512]{2,1,0:T(8,128)(2,1)} %broadcast_in_dim.20), calls=%async_computation.2 | async-start | bytes 1572864 | tf_op jit(solution)/shard_map/all_to_all | solution.py:243
  127.0 2.7 %collective-permute-start.18 = (bf16[32,512]{1,0:T(8,128)(2,1)S(1)}, bf16[32,512]{1,0:T(8,128)(2,1)S(1)}, u32[]{:S(2)}, u32[]{:S(2)}) collective-permute-start(bf16[32,512]{1,0:T(8,128)(2,1)S(1)} %collective-permute-done.17), channel_id=1, source_target_pairs={{0,1},{1,2},{2,3},{3,0},{4,5},{5,6},{6,7},{7,4},{8,9},{9,10},{10,1... | collective-permute-start | bytes 98312 | tf_op jit(solution)/shard_map/ppermute | solution.py:24
  131.4 12.6 %all-to-all-done.2.rest_0_ = bf16[8,96,512]{2,1,0:T(8,128)(2,1)S(1)} async-done(((bf16[8,96,512]{2,1,0:T(8,128)(2,1)}), bf16[8,96,512]{2,1,0:T(8,128)(2,1)S(1)}, u32[]{:S(2)}, u32[]{:S(2)}) %all-to-all-start.2) | async-done | bytes 786464 | tf_op jit(solution)/shard_map/all_to_all | solution.py:243
  146.0 4.5 %all-to-all-start.3 = ((bf16[8,4,32,512]{3,2,1,0:T(8,128)(2,1)}), bf16[8,4,32,512]{3,2,1,0:T(8,128)(2,1)}, u32[]{:S(2)}, u32[]{:S(2)}) async-start(bf16[8,4,32,512]{3,2,1,0:T(8,128)(2,1)} %broadcast_in_dim.21), calls=%async_computation.3 | async-start | bytes 2097152 | tf_op jit(solution)/shard_map/all_to_all | solution.py:243
  152.6 14.9 %collective-permute-done.13.rest_4_ = bf16[8,96,512]{2,1,0:T(8,128)(2,1)S(1)} collective-permute-done((bf16[8,96,512]{2,1,0:T(8,128)(2,1)}, bf16[8,96,512]{2,1,0:T(8,128)(2,1)S(1)}, u32[]{:S(2)}, u32[]{:S(2)}) %collective-permute-start.13) | collective-permute-done | bytes 786464 | tf_op jit(solution)/shard_map/ppermute | solution.py:24
  177.4 4.4 %collective-permute-done.15.rest_3_ = bf16[4,96,512]{2,1,0:T(8,128)(2,1)} collective-permute-done((bf16[4,96,512]{2,1,0:T(8,128)(2,1)}, bf16[4,96,512]{2,1,0:T(8,128)(2,1)}, u32[]{:S(2)}, u32[]{:S(2)}) %collective-permute-start.15) | collective-permute-done | bytes 393248 | tf_op jit(solution)/shard_map/ppermute | solution.py:24
  186.0 8.2 %backward_blocks.1 = (f32[512,512]{1,0:T(8,128)S(1)}, bf16[512,512]{1,0:T(8,128)(2,1)S(1)}) custom-call(s32[256]{0:T(256)S(1)} %select_reduce_fusion.table, bf16[96,128,128]{2,1,0:T(8,128)(2,1)S(1)} %copy-done.3, bf16[8,96,512]{2,1,0:T(8,128)(2,1)S(1)} %copy-done.5, bf16[8,96,512]{2,1,0:T(8,128)(2,1)S(1)} %copy-done.9, ...), custom_call_target="tpu_custom_call" | custom-call | tf_op jit(solution)/shard_map/backward_blocks/pallas_call | solution.py:208
  203.5 2.8 %collective-permute-done.24 = bf16[144,512]{1,0:T(8,128)(2,1)S(1)} collective-permute-done((bf16[144,512]{1,0:T(8,128)(2,1)S(1)}, bf16[144,512]{1,0:T(8,128)(2,1)S(1)}, u32[]{:S(2)}, u32[]{:S(2)}) %collective-permute-start.24) | collective-permute-done | bytes 147488 | tf_op jit(solution)/shard_map/ppermute | solution.py:28
  206.3 3.0 %collective-permute-done.22 = bf16[144,512]{1,0:T(8,128)(2,1)S(1)} collective-permute-done((bf16[144,512]{1,0:T(8,128)(2,1)S(1)}, bf16[144,512]{1,0:T(8,128)(2,1)S(1)}, u32[]{:S(2)}, u32[]{:S(2)}) %collective-permute-start.22) | collective-permute-done | bytes 147488 | tf_op jit(solution)/shard_map/ppermute | solution.py:28
  (130 shorter events, 58.0 us)
Async XLA Ops:
  1.6 6.5 %collective-permute-start.1 = (bf16[128,512]{1,0:T(8,128)(2,1)S(1)}, bf16[128,512]{1,0:T(8,128)(2,1)S(1)}, u32[]{:S(2)}, u32[]{:S(2)}) collective-permute-start(bf16[128,512]{1,0:T(8,128)(2,1)S(1)} %convert_element_type.81), channel_id=1, source_target_pairs={{0,64},{32,96},{64,128},{96,160},{128,192},{160,224},{192,0},{224,... | collective-permute-start | bytes 393224 | tf_op jit(solution)/shard_map/ppermute | solution.py:28
  3.2 5.3 %collective-permute-start = (bf16[128,512]{1,0:T(8,128)(2,1)S(1)}, bf16[128,512]{1,0:T(8,128)(2,1)S(1)}, u32[]{:S(2)}, u32[]{:S(2)}) collective-permute-start(bf16[128,512]{1,0:T(8,128)(2,1)S(1)} %convert_element_type.81), channel_id=1, source_target_pairs={{0,192},{32,224},{64,0},{96,32},{128,64},{160,96},{192,128},{224,1... | collective-permute-start | bytes 393224 | tf_op jit(solution)/shard_map/ppermute | solution.py:28
  8.1 6.2 %collective-permute-start.2 = (bf16[128,512]{1,0:T(8,128)(2,1)S(1)}, bf16[128,512]{1,0:T(8,128)(2,1)S(1)}, u32[]{:S(2)}, u32[]{:S(2)}) collective-permute-start(bf16[128,512]{1,0:T(8,128)(2,1)S(1)} %collective-permute-done.1), channel_id=1, source_target_pairs={{0,64},{32,96},{64,128},{96,160},{128,192},{160,224},{192,0},{224,... | collective-permute-start | bytes 393224 | tf_op jit(solution)/shard_map/ppermute | solution.py:28
  26.5 12.7 %collective-permute-start.6 = (bf16[4,96,512]{2,1,0:T(8,128)(2,1)}, bf16[4,96,512]{2,1,0:T(8,128)(2,1)}, u32[]{:S(2)}, u32[]{:S(2)}) collective-permute-start(bf16[4,96,512]{2,1,0:T(8,128)(2,1)} %get-tuple-element.22), channel_id=1, source_target_pairs={{0,3},{1,0},{2,1},{3,2},{4,7},{5,4},{6,5},{7,6},{8,11},{9,8},{10,9... | collective-permute-start | bytes 1179656 | tf_op jit(solution)/shard_map/ppermute | solution.py:24
  27.2 13.2 %collective-permute-start.4 = (bf16[4,96,512]{2,1,0:T(8,128)(2,1)}, bf16[4,96,512]{2,1,0:T(8,128)(2,1)}, u32[]{:S(2)}, u32[]{:S(2)}) collective-permute-start(bf16[4,96,512]{2,1,0:T(8,128)(2,1)} %get-tuple-element.21), channel_id=1, source_target_pairs={{0,1},{1,2},{2,3},{3,0},{4,5},{5,6},{6,7},{7,4},{8,9},{9,10},{10,1... | collective-permute-start | bytes 1179656 | tf_op jit(solution)/shard_map/ppermute | solution.py:24
  29.7 36.9 %all-to-all-start.1 = ((bf16[8,4,32,512]{3,2,1,0:T(8,128)(2,1)}), bf16[8,4,32,512]{3,2,1,0:T(8,128)(2,1)S(1)}, u32[]{:S(2)}, u32[]{:S(2)}) async-start(bf16[8,4,32,512]{3,2,1,0:T(8,128)(2,1)} %get-tuple-element.14.after), calls=%async_computation.1 | async-start | bytes 2097152 | tf_op jit(solution)/shard_map/all_to_all | solution.py:243
  40.3 20.0 %collective-permute-start.7 = (bf16[8,96,512]{2,1,0:T(8,128)(2,1)S(1)}, bf16[8,96,512]{2,1,0:T(8,128)(2,1)S(1)}, u32[]{:S(2)}, u32[]{:S(2)}) collective-permute-start(bf16[8,96,512]{2,1,0:T(8,128)(2,1)S(1)} %pad_maximum_fusion.1), channel_id=1, source_target_pairs={{0,3},{1,0},{2,1},{3,2},{4,7},{5,4},{6,5},{7,6},{8,11},{9,8},{10,9... | collective-permute-start | bytes 2359304 | tf_op jit(solution)/shard_map/ppermute | solution.py:24
  41.6 19.3 %collective-permute-start.5 = (bf16[8,96,512]{2,1,0:T(8,128)(2,1)S(1)}, bf16[8,96,512]{2,1,0:T(8,128)(2,1)S(1)}, u32[]{:S(2)}, u32[]{:S(2)}) collective-permute-start(bf16[8,96,512]{2,1,0:T(8,128)(2,1)S(1)} %pad_maximum_fusion), channel_id=1, source_target_pairs={{0,1},{1,2},{2,3},{3,0},{4,5},{5,6},{6,7},{7,4},{8,9},{9,10},{10,1... | collective-permute-start | bytes 2359304 | tf_op jit(solution)/shard_map/ppermute | solution.py:24
  66.6 27.0 %all-to-all-start = ((bf16[8,96,512]{2,1,0:T(8,128)(2,1)}), bf16[8,96,512]{2,1,0:T(8,128)(2,1)S(1)}, u32[]{:S(2)}, u32[]{:S(2)}) async-start(bf16[8,96,512]{2,1,0:T(8,128)(2,1)} %add_convert_fusion), calls=%async_computation | async-start | bytes 1572864 | tf_op jit(solution)/shard_map/all_to_all | solution.py:243
  70.7 5.4 %collective-permute-start.8 = (f32[16,512]{1,0:T(8,128)S(1)}, f32[16,512]{1,0:T(8,128)S(1)}, u32[]{:S(2)}, u32[]{:S(2)}) collective-permute-start(f32[16,512]{1,0:T(8,128)S(1)} %get-tuple-element.31), channel_id=1, source_target_pairs={{0,1},{1,2},{2,3},{3,0},{4,5},{5,6},{6,7},{7,4},{8,9},{9,10},{10,1... | collective-permute-start | bytes 98312 | tf_op jit(solution)/shard_map/ppermute | solution.py:24
  74.5 5.1 %collective-permute-start.10 = (f32[16,512]{1,0:T(8,128)S(1)}, f32[16,512]{1,0:T(8,128)S(1)}, u32[]{:S(2)}, u32[]{:S(2)}) collective-permute-start(f32[16,512]{1,0:T(8,128)S(1)} %get-tuple-element.32), channel_id=1, source_target_pairs={{0,3},{1,0},{2,1},{3,2},{4,7},{5,4},{6,5},{7,6},{8,11},{9,8},{10,9... | collective-permute-start | bytes 98312 | tf_op jit(solution)/shard_map/ppermute | solution.py:24
  79.6 5.6 %collective-permute-start.11 = (f32[32,512]{1,0:T(8,128)S(1)}, f32[32,512]{1,0:T(8,128)S(1)}, u32[]{:S(2)}, u32[]{:S(2)}) collective-permute-start(f32[32,512]{1,0:T(8,128)S(1)} %pad_maximum_fusion.8), channel_id=1, source_target_pairs={{0,3},{1,0},{2,1},{3,2},{4,7},{5,4},{6,5},{7,6},{8,11},{9,8},{10,9... | collective-permute-start | bytes 196616 | tf_op jit(solution)/shard_map/ppermute | solution.py:24
  79.7 5.5 %collective-permute-start.9 = (f32[32,512]{1,0:T(8,128)S(1)}, f32[32,512]{1,0:T(8,128)S(1)}, u32[]{:S(2)}, u32[]{:S(2)}) collective-permute-start(f32[32,512]{1,0:T(8,128)S(1)} %pad_maximum_fusion.7), channel_id=1, source_target_pairs={{0,1},{1,2},{2,3},{3,0},{4,5},{5,6},{6,7},{7,4},{8,9},{9,10},{10,1... | collective-permute-start | bytes 196616 | tf_op jit(solution)/shard_map/ppermute | solution.py:24
  96.5 21.9 %all-to-all-start.4 = ((bf16[32,16,512]{2,1,0:T(8,128)(2,1)}), bf16[32,16,512]{2,1,0:T(8,128)(2,1)S(1)}, u32[]{:S(2)}, u32[]{:S(2)}) async-start(bf16[32,16,512]{2,1,0:T(8,128)(2,1)} %bitcast.17), calls=%async_computation.4 | async-start | bytes 1048576 | tf_op jit(solution)/shard_map/all_to_all | solution.py:300
  119.4 24.6 %all-to-all-start.2 = ((bf16[8,96,512]{2,1,0:T(8,128)(2,1)}), bf16[8,96,512]{2,1,0:T(8,128)(2,1)S(1)}, u32[]{:S(2)}, u32[]{:S(2)}) async-start(bf16[8,96,512]{2,1,0:T(8,128)(2,1)} %broadcast_in_dim.20), calls=%async_computation.2 | async-start | bytes 1572864 | tf_op jit(solution)/shard_map/all_to_all | solution.py:243
  124.4 5.4 %collective-permute-start.16 = (bf16[32,512]{1,0:T(8,128)(2,1)S(1)}, bf16[32,512]{1,0:T(8,128)(2,1)S(1)}, u32[]{:S(2)}, u32[]{:S(2)}) collective-permute-start(bf16[32,512]{1,0:T(8,128)(2,1)S(1)} %get-tuple-element.36), channel_id=1, source_target_pairs={{0,3},{1,0},{2,1},{3,2},{4,7},{5,4},{6,5},{7,6},{8,11},{9,8},{10,9... | collective-permute-start | bytes 98312 | tf_op jit(solution)/shard_map/ppermute | solution.py:24
  146.0 30.9 %all-to-all-start.3 = ((bf16[8,4,32,512]{3,2,1,0:T(8,128)(2,1)}), bf16[8,4,32,512]{3,2,1,0:T(8,128)(2,1)}, u32[]{:S(2)}, u32[]{:S(2)}) async-start(bf16[8,4,32,512]{3,2,1,0:T(8,128)(2,1)} %broadcast_in_dim.21), calls=%async_computation.3 | async-start | bytes 2097152 | tf_op jit(solution)/shard_map/all_to_all | solution.py:243
  150.5 17.0 %collective-permute-start.13 = (bf16[8,96,512]{2,1,0:T(8,128)(2,1)}, bf16[8,96,512]{2,1,0:T(8,128)(2,1)S(1)}, u32[]{:S(2)}, u32[]{:S(2)}) collective-permute-start(bf16[8,96,512]{2,1,0:T(8,128)(2,1)} %copy-done.4), channel_id=1, source_target_pairs={{0,1},{1,2},{2,3},{3,0},{4,5},{5,6},{6,7},{7,4},{8,9},{9,10},{10,1... | collective-permute-start | bytes 2359304 | tf_op jit(solution)/shard_map/ppermute | solution.py:24
  151.5 19.3 %collective-permute-start.12 = (bf16[8,96,512]{2,1,0:T(8,128)(2,1)}, bf16[8,96,512]{2,1,0:T(8,128)(2,1)S(1)}, u32[]{:S(2)}, u32[]{:S(2)}) collective-permute-start(bf16[8,96,512]{2,1,0:T(8,128)(2,1)} %copy-done.4), channel_id=1, source_target_pairs={{0,3},{1,0},{2,1},{3,2},{4,7},{5,4},{6,5},{7,6},{8,11},{9,8},{10,9... | collective-permute-start | bytes 2359304 | tf_op jit(solution)/shard_map/ppermute | solution.py:24
  169.3 8.2 %collective-permute-start.14 = (bf16[4,96,512]{2,1,0:T(8,128)(2,1)}, bf16[4,96,512]{2,1,0:T(8,128)(2,1)S(1)}, u32[]{:S(2)}, u32[]{:S(2)}) collective-permute-start(bf16[4,96,512]{2,1,0:T(8,128)(2,1)} %slice.204), channel_id=1, source_target_pairs={{0,1},{1,2},{2,3},{3,0},{4,5},{5,6},{6,7},{7,4},{8,9},{9,10},{10,1... | collective-permute-start | bytes 1179656 | tf_op jit(solution)/shard_map/ppermute | solution.py:24
  172.5 9.3 %collective-permute-start.15 = (bf16[4,96,512]{2,1,0:T(8,128)(2,1)}, bf16[4,96,512]{2,1,0:T(8,128)(2,1)}, u32[]{:S(2)}, u32[]{:S(2)}) collective-permute-start(bf16[4,96,512]{2,1,0:T(8,128)(2,1)} %slice.205), channel_id=1, source_target_pairs={{0,3},{1,0},{2,1},{3,2},{4,7},{5,4},{6,5},{7,6},{8,11},{9,8},{10,9... | collective-permute-start | bytes 1179656 | tf_op jit(solution)/shard_map/ppermute | solution.py:24
  197.1 5.7 %collective-permute-start.21 = (bf16[80,512]{1,0:T(8,128)(2,1)S(1)}, bf16[80,512]{1,0:T(8,128)(2,1)S(1)}, u32[]{:S(2)}, u32[]{:S(2)}) collective-permute-start(bf16[80,512]{1,0:T(8,128)(2,1)S(1)} %get-tuple-element.25), channel_id=1, source_target_pairs={{0,64},{32,96},{64,128},{96,160},{128,192},{160,224},{192,0},{224,... | collective-permute-start | bytes 245768 | tf_op jit(solution)/shard_map/ppermute | solution.py:28
  201.1 5.2 %collective-permute-start.24 = (bf16[144,512]{1,0:T(8,128)(2,1)S(1)}, bf16[144,512]{1,0:T(8,128)(2,1)S(1)}, u32[]{:S(2)}, u32[]{:S(2)}) collective-permute-start(bf16[144,512]{1,0:T(8,128)(2,1)S(1)} %pad_maximum_fusion.5), channel_id=1, source_target_pairs={{0,192},{32,224},{64,0},{96,32},{128,64},{160,96},{192,128},{224,1... | collective-permute-start | bytes 442376 | tf_op jit(solution)/shard_map/ppermute | solution.py:28
  202.9 6.4 %collective-permute-start.22 = (bf16[144,512]{1,0:T(8,128)(2,1)S(1)}, bf16[144,512]{1,0:T(8,128)(2,1)S(1)}, u32[]{:S(2)}, u32[]{:S(2)}) collective-permute-start(bf16[144,512]{1,0:T(8,128)(2,1)S(1)} %pad_maximum_fusion.4), channel_id=1, source_target_pairs={{0,64},{32,96},{64,128},{96,160},{128,192},{160,224},{192,0},{224,... | collective-permute-start | bytes 442376 | tf_op jit(solution)/shard_map/ppermute | solution.py:28
  (23 other events, 132.4 us)

commit v2 on v1

--- a/solution.py
+++ b/solution.py
@@ -10,6 +10,7 @@
 NB = 96
 NX, NC, NZ, NY = 4, 2, 8, 4
 TOP = 96
+NEAR = 80
 PIECES = 2
 F32 = jnp.float32
 BF16 = jnp.bfloat16
@@ -161,24 +162,25 @@
     )(after, vals)
 
 
-def backward_kernel(table, vals, *rest):
-    pieces = rest[: NY + 2]
-    near, away, slope, acc, lhs, sems = rest[NY + 2 :]
+def backward_kernel(table, place, vals, *rest):
+    pieces = rest[: NY + 1 + NZ]
+    near, away, slope, acc, lhs, sems = rest[NY + 1 + NZ :]
     turn = pl.program_id(0)
 
     @pl.when(turn == 0)
     def _():
-        lower, upper = pl.ds(0, TOP), pl.ds(TOP, BLK - TOP)
+        lower, upper = pl.ds(0, NEAR), pl.ds(NEAR, BLK - NEAR)
         cut = NZ // 2
-        y0, y1, y2a, y2b, y3, others = pieces
+        y0, y1, y2a, y2b, y3 = pieces[: NY + 1]
         moves = [
             (y0, slope.at[:, 0, lower]),
             (y1, slope.at[:, 1, lower]),
             (y2a, slope.at[pl.ds(0, cut), 2, lower]),
             (y2b, slope.at[pl.ds(cut, cut), 2, lower]),
             (y3, slope.at[:, 3, lower]),
-            (others, slope.at[:, :, upper]),
         ]
+        for k in range(NZ):
+            moves.append((pieces[NY + 1 + k], slope.at[lax.rem(place[0] + k, NZ), :, upper]))
         copies = [
             pltpu.make_async_copy(src, dst, sems.at[k]) for k, (src, dst) in enumerate(moves)
         ]
@@ -203,12 +205,12 @@
         away[...] = acc[NX * BLK :].astype(BF16)
 
 
-def backward_blocks(table, vals, pieces):
+def backward_blocks(table, place, vals, pieces):
     nodes = NX * NC * BLK
     return pl.pallas_call(
         backward_kernel,
         grid_spec=pltpu.PrefetchScalarGridSpec(
-            num_scalar_prefetch=1,
+            num_scalar_prefetch=2,
             grid=(NZ,),
             in_specs=[whole(NB, BLK, BLK)] + [pl.BlockSpec(memory_space=pltpu.HBM)] * len(pieces),
             out_specs=[whole(NX * BLK, HID), whole(NX * BLK, HID)],
@@ -225,7 +227,23 @@
         ],
         compiler_params=pltpu.CompilerParams(vmem_limit_bytes=20 << 20),
         name="backward_blocks",
-    )(table, vals, *pieces)
+    )(table, place, vals, *pieces)
+
+
+def pull_kernel(slope, high, low, out):
+    left = slope[...].T
+    total = jnp.dot(left, high[...], preferred_element_type=F32)
+    total += jnp.dot(left, low[...], preferred_element_type=F32)
+    out[...] = total.astype(BF16)
+
+
+def pulled(slope, high, low):
+    return pl.pallas_call(
+        pull_kernel,
+        out_shape=jax.ShapeDtypeStruct((HID, HID), BF16),
+        compiler_params=pltpu.CompilerParams(vmem_limit_bytes=6 << 20),
+        name="pulled",
+    )(slope, high, low)
 
 
 def slot_table(block_rows, block_cols, live):
@@ -287,16 +305,13 @@
     slope = cotangent.astype(F32) * sigma * (1.0 + total * (1.0 - sigma))
     slope = slope.astype(BF16)
 
-    top_all = spread(slope[:TOP], ZGROUPS)
-    bottom_all = jnp.stack(ring_gather(slope[TOP:], "y", NY))
+    top_all = spread(slope[:NEAR], ZGROUPS)
+    bottom_all = jnp.stack(ring_gather(slope[NEAR:], "y", NY))
     ypieces = ring_gather(top_all, "y", NY, halves=True)
-    pieces = ypieces + [spread(bottom_all, ZGROUPS)]
+    pieces = ypieces + ring_gather(bottom_all, "z", NZ)
 
     part, width = HID // (NX * NC), HID // (NZ * NY)
-    pull = lambda left: lax.dot_general(
-        slope, left, (((0,), (0,)), ((), ())), preferred_element_type=F32
-    )
-    local = (pull(high) + pull(low)).astype(BF16).reshape(NZ * NY, width, HID)
+    local = pulled(slope, high, low).reshape(NZ * NY, width, HID)
     shares = lax.all_to_all(local, "col", 0, 0, tiled=True)
     shares = jnp.sum(shares.astype(F32), axis=0).reshape(width, NX, NC, part)
     shares = shares.transpose(1, 2, 0, 3).reshape(NX, NC, width * part // HID, HID)
@@ -305,7 +320,7 @@
     other = lax.dynamic_index_in_dim(shares, 1 - core, 1, keepdims=False)
     mine = mine + shift(other, "core", 1)
 
-    near, away = backward_blocks(backward_table, values_t, pieces)
+    near, away = backward_blocks(backward_table, place, values_t, pieces)
     near = near + shift(away, "core", 1).astype(F32)
     spare = jnp.zeros((NX, 16 - mine.shape[1], HID), F32)
     both = jnp.concatenate([near.reshape(NX, BLK, HID), mine, spare], 1)

time: 212 us -> 200 us (0.943)
  the two profiles are of different devices: /device:TPU:24 before, /device:TPU:96 now
where the time goes in v2:
time: 200 us; the launch traced here: 199 us
  starting transfers between devices  79 us (40%)
  waiting for transfers between devices  78.7 us (39%)
  Pallas kernels  17.4 us (9%)
  local copies, waits for them, and re-layouts  13.4 us (7%)
  other arithmetic  7.05 us (4%)
  matrix products  2.28 us (1%)
    ppermute x15, waiting for transfers between devices, shift(): lax.ppermute(value, 'col', [(i, i // NY * NY + (i % NY + step) % NY) for...  34.4 us
    all_to_all x3, starting transfers between devices, exchange(): lax.all_to_all(parts, 'col', 0, 0, axis_index_groups=groups, tiled=True)  23.8 us
    ppermute x15, starting transfers between devices, shift(): lax.ppermute(value, 'col', [(i, i // NY * NY + (i % NY + step) % NY) for...  23.4 us
    ppermute x7, waiting for transfers between devices, shift(): lax.ppermute(value, 'row', [(i, (i // NC + step) % NX * NC + i % NC) for...  17.2 us
    all_to_all x3, waiting for transfers between devices, exchange(): lax.all_to_all(parts, 'col', 0, 0, axis_index_groups=groups, tiled=True)  16 us
    ppermute x7, starting transfers between devices, shift(): lax.ppermute(value, 'col', [(i, (i // NY + step) % NZ * NY + i % NY) for...  13.9 us
    all_to_all x1, starting transfers between devices, on_device(): shares = lax.all_to_all(local, 'col', 0, 0, tiled=True)  9.22 us
    unnamed x27, local copies, waits for them, and re-layouts  9.02 us
  transfers between devices with their start and end apart: 36, of which 21 were waited for; matrix products, arithmetic and copies ran while one was open for 4% of the time, Pallas kernels for 1%

profile of v2, /device:TPU:96, one launch (start us, length us, event | category | flops | bytes accessed | tf_op | source)
XLA Modules:
  0.0 199.0 jit_solution(11732826587505130607)
XLA Ops:
  4.9 3.2 %collective-permute-done.1 = bf16[128,512]{1,0:T(8,128)(2,1)S(1)} collective-permute-done((bf16[128,512]{1,0:T(8,128)(2,1)S(1)}, bf16[128,512]{1,0:T(8,128)(2,1)S(1)}, u32[]{:S(2)}, u32[]{:S(2)}) %collective-permute-start.1) | collective-permute-done | bytes 131104 | tf_op jit(solution)/shard_map/ppermute | solution.py:29
  8.5 5.8 %collective-permute-done.2 = bf16[128,512]{1,0:T(8,128)(2,1)S(1)} collective-permute-done((bf16[128,512]{1,0:T(8,128)(2,1)S(1)}, bf16[128,512]{1,0:T(8,128)(2,1)S(1)}, u32[]{:S(2)}, u32[]{:S(2)}) %collective-permute-start.2) | collective-permute-done | bytes 131104 | tf_op jit(solution)/shard_map/ppermute | solution.py:29
  18.2 7.3 %forward_blocks.1 = (bf16[8,96,512]{2,1,0:T(8,128)(2,1)S(1)}, bf16[8,96,512]{2,1,0:T(8,128)(2,1)S(1)}, bf16[8,96,512]{2,1,0:T(8,128)(2,1)S(1)}, bf16[8,96,512]{2,1,0:T(8,128)(2,1)S(1)}, bf16[8,4,32,512]{3,2,1,0:T(8,128)(2,1)}) custom-call(s32[256]{0:T(256)S(1)} %select_reduce_fusion.1.table, s32[2]{0:T(128)S(1)} %pad_add_fusion.place, ...), custom_call_target="tpu_custom_call" | custom-call | tf_op jit(solution)/shard_map/forward_blocks/pallas_call | solution.py:122
  29.5 7.7 %all-to-all-start.1 = ((bf16[8,4,32,512]{3,2,1,0:T(8,128)(2,1)}), bf16[8,4,32,512]{3,2,1,0:T(8,128)(2,1)S(1)}, u32[]{:S(2)}, u32[]{:S(2)}) async-start(bf16[8,4,32,512]{3,2,1,0:T(8,128)(2,1)} %get-tuple-element.14.after), calls=%async_computation.1 | async-start | bytes 2097152 | tf_op jit(solution)/shard_map/all_to_all | solution.py:261
  39.6 3.8 %collective-permute-start.7 = (bf16[8,96,512]{2,1,0:T(8,128)(2,1)S(1)}, bf16[8,96,512]{2,1,0:T(8,128)(2,1)S(1)}, u32[]{:S(2)}, u32[]{:S(2)}) collective-permute-start(bf16[8,96,512]{2,1,0:T(8,128)(2,1)S(1)} %pad_maximum_fusion.1), channel_id=1, source_target_pairs={{0,3},{1,0},{2,1},{3,2},{4,7},{5,4},{6,5},{7,6},{8,11},{9,8},{10,9... | collective-permute-start | bytes 2359304 | tf_op jit(solution)/shard_map/ppermute | solution.py:25
  44.7 15.0 %collective-permute-done.7 = bf16[8,96,512]{2,1,0:T(8,128)(2,1)S(1)} collective-permute-done((bf16[8,96,512]{2,1,0:T(8,128)(2,1)S(1)}, bf16[8,96,512]{2,1,0:T(8,128)(2,1)S(1)}, u32[]{:S(2)}, u32[]{:S(2)}) %collective-permute-start.7) | collective-permute-done | bytes 786464 | tf_op jit(solution)/shard_map/ppermute | solution.py:25
  59.7 4.7 %collective-permute-done.5 = bf16[8,96,512]{2,1,0:T(8,128)(2,1)S(1)} collective-permute-done((bf16[8,96,512]{2,1,0:T(8,128)(2,1)S(1)}, bf16[8,96,512]{2,1,0:T(8,128)(2,1)S(1)}, u32[]{:S(2)}, u32[]{:S(2)}) %collective-permute-start.5) | collective-permute-done | bytes 786464 | tf_op jit(solution)/shard_map/ppermute | solution.py:25
  65.6 7.7 %all-to-all-start = ((bf16[8,96,512]{2,1,0:T(8,128)(2,1)}), bf16[8,96,512]{2,1,0:T(8,128)(2,1)S(1)}, u32[]{:S(2)}, u32[]{:S(2)}) async-start(bf16[8,96,512]{2,1,0:T(8,128)(2,1)} %add_convert_fusion), calls=%async_computation | async-start | bytes 1572864 | tf_op jit(solution)/shard_map/all_to_all | solution.py:261
  73.5 3.2 %collective-permute-start.10 = (f32[16,512]{1,0:T(8,128)S(1)}, f32[16,512]{1,0:T(8,128)S(1)}, u32[]{:S(2)}, u32[]{:S(2)}) collective-permute-start(f32[16,512]{1,0:T(8,128)S(1)} %get-tuple-element.32), channel_id=1, source_target_pairs={{0,3},{1,0},{2,1},{3,2},{4,7},{5,4},{6,5},{7,6},{8,11},{9,8},{10,9... | collective-permute-start | bytes 98312 | tf_op jit(solution)/shard_map/ppermute | solution.py:25
  78.6 3.3 %collective-permute-start.11 = (f32[32,512]{1,0:T(8,128)S(1)}, f32[32,512]{1,0:T(8,128)S(1)}, u32[]{:S(2)}, u32[]{:S(2)}) collective-permute-start(f32[32,512]{1,0:T(8,128)S(1)} %pad_maximum_fusion.8), channel_id=1, source_target_pairs={{0,3},{1,0},{2,1},{3,2},{4,7},{5,4},{6,5},{7,6},{8,11},{9,8},{10,9... | collective-permute-start | bytes 196616 | tf_op jit(solution)/shard_map/ppermute | solution.py:25
  83.9 3.6 %collective-permute-done.9 = f32[32,512]{1,0:T(8,128)S(1)} collective-permute-done((f32[32,512]{1,0:T(8,128)S(1)}, f32[32,512]{1,0:T(8,128)S(1)}, u32[]{:S(2)}, u32[]{:S(2)}) %collective-permute-start.9) | collective-permute-done | bytes 65568 | tf_op jit(solution)/shard_map/ppermute | solution.py:25
  92.7 8.4 %all-to-all-start.2 = ((bf16[8,80,512]{2,1,0:T(8,128)(2,1)}), bf16[8,80,512]{2,1,0:T(8,128)(2,1)}, u32[]{:S(2)}, u32[]{:S(2)}) async-start(bf16[8,80,512]{2,1,0:T(8,128)(2,1)} %broadcast_in_dim.17), calls=%async_computation.2 | async-start | bytes 1310720 | tf_op jit(solution)/shard_map/all_to_all | solution.py:261
  102.4 13.1 %all-to-all-done.2.rest_0_ = bf16[8,80,512]{2,1,0:T(8,128)(2,1)} async-done(((bf16[8,80,512]{2,1,0:T(8,128)(2,1)}), bf16[8,80,512]{2,1,0:T(8,128)(2,1)}, u32[]{:S(2)}, u32[]{:S(2)}) %all-to-all-start.2) | async-done | bytes 655392 | tf_op jit(solution)/shard_map/all_to_all | solution.py:261
  115.5 9.2 %all-to-all-start.3 = ((bf16[32,16,512]{2,1,0:T(8,128)(2,1)}), bf16[32,16,512]{2,1,0:T(8,128)(2,1)}, u32[]{:S(2)}, u32[]{:S(2)}) async-start(bf16[32,16,512]{2,1,0:T(8,128)(2,1)} %bitcast.97), calls=%async_computation.3 | async-start | bytes 1048576 | tf_op jit(solution)/shard_map/all_to_all | solution.py:315
  134.0 3.5 %collective-permute-done.18 = bf16[48,512]{1,0:T(8,128)(2,1)S(1)} collective-permute-done((bf16[48,512]{1,0:T(8,128)(2,1)S(1)}, bf16[48,512]{1,0:T(8,128)(2,1)S(1)}, u32[]{:S(2)}, u32[]{:S(2)}) %collective-permute-start.18) | collective-permute-done | bytes 49184 | tf_op jit(solution)/shard_map/ppermute | solution.py:25
  137.6 3.2 %collective-permute-start.22 = (bf16[4,48,512]{2,1,0:T(8,128)(2,1)S(1)}, bf16[4,48,512]{2,1,0:T(8,128)(2,1)S(1)}, u32[]{:S(2)}, u32[]{:S(2)}) collective-permute-start(bf16[4,48,512]{2,1,0:T(8,128)(2,1)S(1)} %pad_maximum_fusion.4.rest_5_), channel_id=1, source_target_pairs={{0,4},{1,5},{2,6},{3,7},{4,8},{5,9},{6,10},{7,11},{8,12},{9,13},{1... | collective-permute-start | bytes 589832 | tf_op jit(solution)/shard_map/ppermute | solution.py:21
  140.8 3.7 %collective-permute-done.22.rest_12_ = bf16[4,48,512]{2,1,0:T(8,128)(2,1)S(1)} collective-permute-done((bf16[4,48,512]{2,1,0:T(8,128)(2,1)S(1)}, bf16[4,48,512]{2,1,0:T(8,128)(2,1)S(1)}, u32[]{:S(2)}, u32[]{:S(2)}) %collective-permute-start.22) | collective-permute-done | bytes 196640 | tf_op jit(solution)/shard_map/ppermute | solution.py:21
  144.5 3.7 %collective-permute-start.23 = (bf16[4,48,512]{2,1,0:T(8,128)(2,1)S(1)}, bf16[4,48,512]{2,1,0:T(8,128)(2,1)}, u32[]{:S(2)}, u32[]{:S(2)}) collective-permute-start(bf16[4,48,512]{2,1,0:T(8,128)(2,1)S(1)} %collective-permute-done.22.rest_12_), channel_id=1, source_target_pairs={{0,4},{1,5},{2,6},{3,7},{4,8},{5,9},{6,10},{7,11},{8,12},{9,13},{1... | collective-permute-start | bytes 589832 | tf_op jit(solution)/shard_map/ppermute | solution.py:21
  148.4 4.2 %collective-permute-done.23.rest_11_ = bf16[4,48,512]{2,1,0:T(8,128)(2,1)} collective-permute-done((bf16[4,48,512]{2,1,0:T(8,128)(2,1)S(1)}, bf16[4,48,512]{2,1,0:T(8,128)(2,1)}, u32[]{:S(2)}, u32[]{:S(2)}) %collective-permute-start.23) | collective-permute-done | bytes 196640 | tf_op jit(solution)/shard_map/ppermute | solution.py:21
  152.6 3.8 %collective-permute-start.24 = (bf16[4,48,512]{2,1,0:T(8,128)(2,1)}, bf16[4,48,512]{2,1,0:T(8,128)(2,1)}, u32[]{:S(2)}, u32[]{:S(2)}) collective-permute-start(bf16[4,48,512]{2,1,0:T(8,128)(2,1)} %collective-permute-done.23.rest_11_), channel_id=1, source_target_pairs={{0,4},{1,5},{2,6},{3,7},{4,8},{5,9},{6,10},{7,11},{8,12},{9,13},{1... | collective-permute-start | bytes 589832 | tf_op jit(solution)/shard_map/ppermute | solution.py:21
  159.6 3.2 %collective-permute-start.15 = (bf16[4,80,512]{2,1,0:T(8,128)(2,1)}, bf16[4,80,512]{2,1,0:T(8,128)(2,1)}, u32[]{:S(2)}, u32[]{:S(2)}) collective-permute-start(bf16[4,80,512]{2,1,0:T(8,128)(2,1)} %slice.205), channel_id=1, source_target_pairs={{0,3},{1,0},{2,1},{3,2},{4,7},{5,4},{6,5},{7,6},{8,11},{9,8},{10,9... | collective-permute-start | bytes 983048 | tf_op jit(solution)/shard_map/ppermute | solution.py:25
  162.8 3.2 %collective-permute-start.25 = (bf16[4,48,512]{2,1,0:T(8,128)(2,1)}, bf16[4,48,512]{2,1,0:T(8,128)(2,1)}, u32[]{:S(2)}, u32[]{:S(2)}) collective-permute-start(bf16[4,48,512]{2,1,0:T(8,128)(2,1)} %collective-permute-done.24.rest_10_), channel_id=1, source_target_pairs={{0,4},{1,5},{2,6},{3,7},{4,8},{5,9},{6,10},{7,11},{8,12},{9,13},{1... | collective-permute-start | bytes 589832 | tf_op jit(solution)/shard_map/ppermute | solution.py:21
  173.6 8.4 %backward_blocks.1 = (f32[512,512]{1,0:T(8,128)S(1)}, bf16[512,512]{1,0:T(8,128)(2,1)S(1)}) custom-call(s32[256]{0:T(256)S(1)} %select_reduce_fusion.table, s32[2]{0:T(128)S(1)} %pad_add_fusion.place, bf16[96,128,128]{2,1,0:T(8,128)(2,1)S(1)} %copy-done.3, bf16[8,80,512]{2,1,0:T(8,128)(2,1)} %all-to-all-done.2.rest_0_, bf16[8,80,512]{2,1,0:T(8,128)(2,1)S(1)} %copy-done.8, ...), custom_call_target="tpu_custom_call" | custom-call | tf_op jit(solution)/shard_map/backward_blocks/pallas_call | solution.py:210
  194.2 3.0 %collective-permute-done.29 = bf16[144,512]{1,0:T(8,128)(2,1)S(1)} collective-permute-done((bf16[144,512]{1,0:T(8,128)(2,1)S(1)}, bf16[144,512]{1,0:T(8,128)(2,1)S(1)}, u32[]{:S(2)}, u32[]{:S(2)}) %collective-permute-start.29) | collective-permute-done | bytes 147488 | tf_op jit(solution)/shard_map/ppermute | solution.py:29
  (134 shorter events, 61.9 us)
Async XLA Ops:
  1.6 6.5 %collective-permute-start.1 = (bf16[128,512]{1,0:T(8,128)(2,1)S(1)}, bf16[128,512]{1,0:T(8,128)(2,1)S(1)}, u32[]{:S(2)}, u32[]{:S(2)}) collective-permute-start(bf16[128,512]{1,0:T(8,128)(2,1)S(1)} %convert_element_type.78), channel_id=1, source_target_pairs={{0,64},{32,96},{64,128},{96,160},{128,192},{160,224},{192,0},{224,... | collective-permute-start | bytes 393224 | tf_op jit(solution)/shard_map/ppermute | solution.py:29
  8.1 6.2 %collective-permute-start.2 = (bf16[128,512]{1,0:T(8,128)(2,1)S(1)}, bf16[128,512]{1,0:T(8,128)(2,1)S(1)}, u32[]{:S(2)}, u32[]{:S(2)}) collective-permute-start(bf16[128,512]{1,0:T(8,128)(2,1)S(1)} %collective-permute-done.1), channel_id=1, source_target_pairs={{0,64},{32,96},{64,128},{96,160},{128,192},{160,224},{192,0},{224,... | collective-permute-start | bytes 393224 | tf_op jit(solution)/shard_map/ppermute | solution.py:29
  26.5 12.0 %collective-permute-start.6 = (bf16[4,96,512]{2,1,0:T(8,128)(2,1)}, bf16[4,96,512]{2,1,0:T(8,128)(2,1)}, u32[]{:S(2)}, u32[]{:S(2)}) collective-permute-start(bf16[4,96,512]{2,1,0:T(8,128)(2,1)} %get-tuple-element.22), channel_id=1, source_target_pairs={{0,3},{1,0},{2,1},{3,2},{4,7},{5,4},{6,5},{7,6},{8,11},{9,8},{10,9... | collective-permute-start | bytes 1179656 | tf_op jit(solution)/shard_map/ppermute | solution.py:25
  29.5 13.9 %collective-permute-start.4 = (bf16[4,96,512]{2,1,0:T(8,128)(2,1)}, bf16[4,96,512]{2,1,0:T(8,128)(2,1)}, u32[]{:S(2)}, u32[]{:S(2)}) collective-permute-start(bf16[4,96,512]{2,1,0:T(8,128)(2,1)} %get-tuple-element.21), channel_id=1, source_target_pairs={{0,1},{1,2},{2,3},{3,0},{4,5},{5,6},{6,7},{7,4},{8,9},{9,10},{10,1... | collective-permute-start | bytes 1179656 | tf_op jit(solution)/shard_map/ppermute | solution.py:25
  29.5 36.1 %all-to-all-start.1 = ((bf16[8,4,32,512]{3,2,1,0:T(8,128)(2,1)}), bf16[8,4,32,512]{3,2,1,0:T(8,128)(2,1)S(1)}, u32[]{:S(2)}, u32[]{:S(2)}) async-start(bf16[8,4,32,512]{3,2,1,0:T(8,128)(2,1)} %get-tuple-element.14.after), calls=%async_computation.1 | async-start | bytes 2097152 | tf_op jit(solution)/shard_map/all_to_all | solution.py:261
  39.6 20.0 %collective-permute-start.7 = (bf16[8,96,512]{2,1,0:T(8,128)(2,1)S(1)}, bf16[8,96,512]{2,1,0:T(8,128)(2,1)S(1)}, u32[]{:S(2)}, u32[]{:S(2)}) collective-permute-start(bf16[8,96,512]{2,1,0:T(8,128)(2,1)S(1)} %pad_maximum_fusion.1), channel_id=1, source_target_pairs={{0,3},{1,0},{2,1},{3,2},{4,7},{5,4},{6,5},{7,6},{8,11},{9,8},{10,9... | collective-permute-start | bytes 2359304 | tf_op jit(solution)/shard_map/ppermute | solution.py:25
  44.6 19.7 %collective-permute-start.5 = (bf16[8,96,512]{2,1,0:T(8,128)(2,1)S(1)}, bf16[8,96,512]{2,1,0:T(8,128)(2,1)S(1)}, u32[]{:S(2)}, u32[]{:S(2)}) collective-permute-start(bf16[8,96,512]{2,1,0:T(8,128)(2,1)S(1)} %pad_maximum_fusion), channel_id=1, source_target_pairs={{0,1},{1,2},{2,3},{3,0},{4,5},{5,6},{6,7},{7,4},{8,9},{9,10},{10,1... | collective-permute-start | bytes 2359304 | tf_op jit(solution)/shard_map/ppermute | solution.py:25
  65.6 24.8 %all-to-all-start = ((bf16[8,96,512]{2,1,0:T(8,128)(2,1)}), bf16[8,96,512]{2,1,0:T(8,128)(2,1)S(1)}, u32[]{:S(2)}, u32[]{:S(2)}) async-start(bf16[8,96,512]{2,1,0:T(8,128)(2,1)} %add_convert_fusion), calls=%async_computation | async-start | bytes 1572864 | tf_op jit(solution)/shard_map/all_to_all | solution.py:261
  92.7 22.8 %all-to-all-start.2 = ((bf16[8,80,512]{2,1,0:T(8,128)(2,1)}), bf16[8,80,512]{2,1,0:T(8,128)(2,1)}, u32[]{:S(2)}, u32[]{:S(2)}) async-start(bf16[8,80,512]{2,1,0:T(8,128)(2,1)} %broadcast_in_dim.17), calls=%async_computation.2 | async-start | bytes 1310720 | tf_op jit(solution)/shard_map/all_to_all | solution.py:261
  115.5 53.7 %all-to-all-start.3 = ((bf16[32,16,512]{2,1,0:T(8,128)(2,1)}), bf16[32,16,512]{2,1,0:T(8,128)(2,1)}, u32[]{:S(2)}, u32[]{:S(2)}) async-start(bf16[32,16,512]{2,1,0:T(8,128)(2,1)} %bitcast.97), calls=%async_computation.3 | async-start | bytes 1048576 | tf_op jit(solution)/shard_map/all_to_all | solution.py:315
  126.3 7.7 %collective-permute-start.16 = (bf16[48,512]{1,0:T(8,128)(2,1)S(1)}, bf16[48,512]{1,0:T(8,128)(2,1)S(1)}, u32[]{:S(2)}, u32[]{:S(2)}) collective-permute-start(bf16[48,512]{1,0:T(8,128)(2,1)S(1)} %get-tuple-element.36), channel_id=1, source_target_pairs={{0,3},{1,0},{2,1},{3,2},{4,7},{5,4},{6,5},{7,6},{8,11},{9,8},{10,9... | collective-permute-start | bytes 147464 | tf_op jit(solution)/shard_map/ppermute | solution.py:25
  130.7 6.9 %collective-permute-start.18 = (bf16[48,512]{1,0:T(8,128)(2,1)S(1)}, bf16[48,512]{1,0:T(8,128)(2,1)S(1)}, u32[]{:S(2)}, u32[]{:S(2)}) collective-permute-start(bf16[48,512]{1,0:T(8,128)(2,1)S(1)} %collective-permute-done.17), channel_id=1, source_target_pairs={{0,1},{1,2},{2,3},{3,0},{4,5},{5,6},{6,7},{7,4},{8,9},{9,10},{10,1... | collective-permute-start | bytes 147464 | tf_op jit(solution)/shard_map/ppermute | solution.py:25
  130.8 25.6 %collective-permute-start.13 = (bf16[8,80,512]{2,1,0:T(8,128)(2,1)}, bf16[8,80,512]{2,1,0:T(8,128)(2,1)S(1)}, u32[]{:S(2)}, u32[]{:S(2)}) collective-permute-start(bf16[8,80,512]{2,1,0:T(8,128)(2,1)} %all-to-all-done.2.rest_0_), channel_id=1, source_target_pairs={{0,1},{1,2},{2,3},{3,0},{4,5},{5,6},{6,7},{7,4},{8,9},{9,10},{10,1... | collective-permute-start | bytes 1966088 | tf_op jit(solution)/shard_map/ppermute | solution.py:25
  132.5 25.5 %collective-permute-start.12 = (bf16[8,80,512]{2,1,0:T(8,128)(2,1)}, bf16[8,80,512]{2,1,0:T(8,128)(2,1)S(1)}, u32[]{:S(2)}, u32[]{:S(2)}) collective-permute-start(bf16[8,80,512]{2,1,0:T(8,128)(2,1)} %all-to-all-done.2.rest_0_), channel_id=1, source_target_pairs={{0,3},{1,0},{2,1},{3,2},{4,7},{5,4},{6,5},{7,6},{8,11},{9,8},{10,9... | collective-permute-start | bytes 1966088 | tf_op jit(solution)/shard_map/ppermute | solution.py:25
  137.6 6.9 %collective-permute-start.22 = (bf16[4,48,512]{2,1,0:T(8,128)(2,1)S(1)}, bf16[4,48,512]{2,1,0:T(8,128)(2,1)S(1)}, u32[]{:S(2)}, u32[]{:S(2)}) collective-permute-start(bf16[4,48,512]{2,1,0:T(8,128)(2,1)S(1)} %pad_maximum_fusion.4.rest_5_), channel_id=1, source_target_pairs={{0,4},{1,5},{2,6},{3,7},{4,8},{5,9},{6,10},{7,11},{8,12},{9,13},{1... | collective-permute-start | bytes 589832 | tf_op jit(solution)/shard_map/ppermute | solution.py:21
  140.8 7.6 %collective-permute-start.19 = (bf16[4,48,512]{2,1,0:T(8,128)(2,1)S(1)}, bf16[4,48,512]{2,1,0:T(8,128)(2,1)}, u32[]{:S(2)}, u32[]{:S(2)}) collective-permute-start(bf16[4,48,512]{2,1,0:T(8,128)(2,1)S(1)} %pad_maximum_fusion.4.rest_5_), channel_id=1, source_target_pairs={{0,28},{1,29},{2,30},{3,31},{4,0},{5,1},{6,2},{7,3},{8,4},{9,5},{1... | collective-permute-start | bytes 589832 | tf_op jit(solution)/shard_map/ppermute | solution.py:21
  144.5 8.1 %collective-permute-start.23 = (bf16[4,48,512]{2,1,0:T(8,128)(2,1)S(1)}, bf16[4,48,512]{2,1,0:T(8,128)(2,1)}, u32[]{:S(2)}, u32[]{:S(2)}) collective-permute-start(bf16[4,48,512]{2,1,0:T(8,128)(2,1)S(1)} %collective-permute-done.22.rest_12_), channel_id=1, source_target_pairs={{0,4},{1,5},{2,6},{3,7},{4,8},{5,9},{6,10},{7,11},{8,12},{9,13},{1... | collective-permute-start | bytes 589832 | tf_op jit(solution)/shard_map/ppermute | solution.py:21
  148.4 14.5 %collective-permute-start.20 = (bf16[4,48,512]{2,1,0:T(8,128)(2,1)}, bf16[4,48,512]{2,1,0:T(8,128)(2,1)}, u32[]{:S(2)}, u32[]{:S(2)}) collective-permute-start(bf16[4,48,512]{2,1,0:T(8,128)(2,1)} %collective-permute-done.19.rest_6_), channel_id=1, source_target_pairs={{0,28},{1,29},{2,30},{3,31},{4,0},{5,1},{6,2},{7,3},{8,4},{9,5},{1... | collective-permute-start | bytes 589832 | tf_op jit(solution)/shard_map/ppermute | solution.py:21
  152.6 10.3 %collective-permute-start.24 = (bf16[4,48,512]{2,1,0:T(8,128)(2,1)}, bf16[4,48,512]{2,1,0:T(8,128)(2,1)}, u32[]{:S(2)}, u32[]{:S(2)}) collective-permute-start(bf16[4,48,512]{2,1,0:T(8,128)(2,1)} %collective-permute-done.23.rest_11_), channel_id=1, source_target_pairs={{0,4},{1,5},{2,6},{3,7},{4,8},{5,9},{6,10},{7,11},{8,12},{9,13},{1... | collective-permute-start | bytes 589832 | tf_op jit(solution)/shard_map/ppermute | solution.py:21
  158.0 12.6 %collective-permute-start.14 = (bf16[4,80,512]{2,1,0:T(8,128)(2,1)}, bf16[4,80,512]{2,1,0:T(8,128)(2,1)}, u32[]{:S(2)}, u32[]{:S(2)}) collective-permute-start(bf16[4,80,512]{2,1,0:T(8,128)(2,1)} %slice.204), channel_id=1, source_target_pairs={{0,1},{1,2},{2,3},{3,0},{4,5},{5,6},{6,7},{7,4},{8,9},{9,10},{10,1... | collective-permute-start | bytes 983048 | tf_op jit(solution)/shard_map/ppermute | solution.py:25
  159.6 11.0 %collective-permute-start.15 = (bf16[4,80,512]{2,1,0:T(8,128)(2,1)}, bf16[4,80,512]{2,1,0:T(8,128)(2,1)}, u32[]{:S(2)}, u32[]{:S(2)}) collective-permute-start(bf16[4,80,512]{2,1,0:T(8,128)(2,1)} %slice.205), channel_id=1, source_target_pairs={{0,3},{1,0},{2,1},{3,2},{4,7},{5,4},{6,5},{7,6},{8,11},{9,8},{10,9... | collective-permute-start | bytes 983048 | tf_op jit(solution)/shard_map/ppermute | solution.py:25
  162.8 7.7 %collective-permute-start.21 = (bf16[4,48,512]{2,1,0:T(8,128)(2,1)}, bf16[4,48,512]{2,1,0:T(8,128)(2,1)}, u32[]{:S(2)}, u32[]{:S(2)}) collective-permute-start(bf16[4,48,512]{2,1,0:T(8,128)(2,1)} %collective-permute-done.20.rest_7_), channel_id=1, source_target_pairs={{0,28},{1,29},{2,30},{3,31},{4,0},{5,1},{6,2},{7,3},{8,4},{9,5},{1... | collective-permute-start | bytes 589832 | tf_op jit(solution)/shard_map/ppermute | solution.py:21
  162.8 7.7 %collective-permute-start.25 = (bf16[4,48,512]{2,1,0:T(8,128)(2,1)}, bf16[4,48,512]{2,1,0:T(8,128)(2,1)}, u32[]{:S(2)}, u32[]{:S(2)}) collective-permute-start(bf16[4,48,512]{2,1,0:T(8,128)(2,1)} %collective-permute-done.24.rest_10_), channel_id=1, source_target_pairs={{0,4},{1,5},{2,6},{3,7},{4,8},{5,9},{6,10},{7,11},{8,12},{9,13},{1... | collective-permute-start | bytes 589832 | tf_op jit(solution)/shard_map/ppermute | solution.py:21
  190.8 6.4 %collective-permute-start.29 = (bf16[144,512]{1,0:T(8,128)(2,1)S(1)}, bf16[144,512]{1,0:T(8,128)(2,1)S(1)}, u32[]{:S(2)}, u32[]{:S(2)}) collective-permute-start(bf16[144,512]{1,0:T(8,128)(2,1)S(1)} %pad_maximum_fusion.5), channel_id=1, source_target_pairs={{0,64},{32,96},{64,128},{96,160},{128,192},{160,224},{192,0},{224,... | collective-permute-start | bytes 442376 | tf_op jit(solution)/shard_map/ppermute | solution.py:29
  (25 other events, 175.9 us)

commit v3 on v2

--- a/solution.py
+++ b/solution.py
@@ -84,18 +84,31 @@
     return pl.BlockSpec(shape, lambda *_: (0,) * len(shape), pipeline_mode=pl.Buffered(1))
 
 
-def forward_kernel(table, place, vals, *rest):
+def fill_rows(table, turn, vals, lhs):
+    for k in range(NY):
+        for j in range(NX * NC):
+            fill_tile(table[(turn * NY + k) * NX * NC + j], vals, lhs, k * BLK, j * BLK)
+
+
+def fill_columns(table, turn, vals, lhs):
+    for j in range(NX * NC):
+        for k in range(NY):
+            fill_tile(table[(turn * NY + k) * NX * NC + j], vals, lhs, j * BLK, k * BLK)
+
+
+def in_turns(table, vals, fill, tiles, multiply):
+    turn = pl.program_id(0) * 2
+    fill(table, turn + 1, vals, tiles[1])
+    multiply(turn, 0, tiles[0])
+    fill(table, jnp.minimum(turn + 2, NZ - 1), vals, tiles[0])
+    multiply(turn + 1, 1, tiles[1])
+
+
+def forward_kernel(table, vals, *rest):
     pieces = rest[:PIECES]
-    y0, y1, y2, y3, zo, gathered, lhs, sems = rest[PIECES:]
-    turn = pl.program_id(0)
-
-    def tile_rows(turn):
-        for k in range(NY):
-            for j in range(NX * NC):
-                slot = table[(turn * NY + k) * NX * NC + j]
-                fill_tile(slot, vals, lhs, k * BLK, j * BLK)
-
-    @pl.when(turn == 0)
+    y0, y1, y2, y3, zo, gathered, even, odd, sems = rest[PIECES:]
+
+    @pl.when(pl.program_id(0) == 0)
     def _():
         copies, start = [], 0
         for k, piece in enumerate(pieces):
@@ -106,40 +119,41 @@
             start += count
         for copy in copies:
             copy.start()
+        fill_rows(table, 0, vals, even)
         for copy in copies:
             copy.wait()
 
-    tile_rows(turn)
-    out = jnp.dot(lhs[...], gathered[...], preferred_element_type=F32).astype(BF16)
-    for k, y in enumerate((y0, y1, y2, y3)):
-        y[0] = out[k * BLK : k * BLK + TOP]
-        zo[0, k] = out[k * BLK + TOP : (k + 1) * BLK]
-
-
-def forward_blocks(table, place, vals, pieces):
-    yspec = pl.BlockSpec((1, TOP, HID), lambda g, t, p: (lax.rem(g + p[0], NZ), 0, 0))
+    def multiply(turn, n, lhs):
+        out = jnp.dot(lhs[...], gathered[...], preferred_element_type=F32).astype(BF16)
+        for k, y in enumerate((y0, y1, y2, y3)):
+            y[n] = out[k * BLK : k * BLK + TOP]
+            zo[n, k] = out[k * BLK + TOP : (k + 1) * BLK]
+
+    in_turns(table, vals, fill_rows, (even, odd), multiply)
+
+
+def forward_blocks(table, vals, pieces):
     nodes = NX * NC * BLK
     return pl.pallas_call(
         forward_kernel,
         grid_spec=pltpu.PrefetchScalarGridSpec(
-            num_scalar_prefetch=2,
-            grid=(NZ,),
+            num_scalar_prefetch=1,
+            grid=(NZ // 2,),
             in_specs=[whole(NB, BLK, BLK)] + [pl.BlockSpec(memory_space=pltpu.HBM)] * len(pieces),
-            out_specs=[yspec] * NY
-            + [pl.BlockSpec(
-                (1, NY, BLK - TOP, HID), lambda g, t, p: (lax.rem(g + p[0], NZ), 0, 0, 0)
-            )],
+            out_specs=[pl.BlockSpec((2, TOP, HID), lambda g, t: (g, 0, 0))] * NY
+            + [pl.BlockSpec((2, NY, BLK - TOP, HID), lambda g, t: (g, 0, 0, 0))],
             scratch_shapes=[
                 pltpu.VMEM((nodes, HID), BF16),
+                pltpu.VMEM((NY * BLK, nodes), BF16),
                 pltpu.VMEM((NY * BLK, nodes), BF16),
                 pltpu.SemaphoreType.DMA((len(pieces),)),
             ],
         ),
         out_shape=[jax.ShapeDtypeStruct((NZ, TOP, HID), BF16)] * NY
         + [jax.ShapeDtypeStruct((NZ, NY, BLK - TOP, HID), BF16)],
-        compiler_params=pltpu.CompilerParams(vmem_limit_bytes=16 << 20),
+        compiler_params=pltpu.CompilerParams(vmem_limit_bytes=20 << 20),
         name="forward_blocks",
-    )(table, place, vals, *pieces)
+    )(table, vals, *pieces)
 
 
 def turn_kernel(after, vals, vals_t):
@@ -164,10 +178,9 @@
 
 def backward_kernel(table, place, vals, *rest):
     pieces = rest[: NY + 1 + NZ]
-    near, away, slope, acc, lhs, sems = rest[NY + 1 + NZ :]
-    turn = pl.program_id(0)
-
-    @pl.when(turn == 0)
+    near, away, slope, acc, even, odd, sems = rest[NY + 1 + NZ :]
+
+    @pl.when(pl.program_id(0) == 0)
     def _():
         lower, upper = pl.ds(0, NEAR), pl.ds(NEAR, BLK - NEAR)
         cut = NZ // 2
@@ -187,19 +200,18 @@
         for copy in copies:
             copy.start()
         acc[...] = jnp.zeros_like(acc)
+        fill_columns(table, 0, vals, even)
         for copy in copies:
             copy.wait()
 
-    for j in range(NX * NC):
-        for k in range(NY):
-            slot = table[(turn * NY + k) * NX * NC + j]
-            fill_tile(slot, vals, lhs, j * BLK, k * BLK)
-
-    acc[...] += jnp.dot(
-        lhs[...], slope[turn].reshape(NY * BLK, HID), preferred_element_type=F32
-    )
-
-    @pl.when(turn == NZ - 1)
+    def multiply(turn, n, lhs):
+        acc[...] += jnp.dot(
+            lhs[...], slope[turn].reshape(NY * BLK, HID), preferred_element_type=F32
+        )
+
+    in_turns(table, vals, fill_columns, (even, odd), multiply)
+
+    @pl.when(pl.program_id(0) == NZ // 2 - 1)
     def _():
         near[...] = acc[: NX * BLK]
         away[...] = acc[NX * BLK :].astype(BF16)
@@ -211,12 +223,13 @@
         backward_kernel,
         grid_spec=pltpu.PrefetchScalarGridSpec(
             num_scalar_prefetch=2,
-            grid=(NZ,),
+            grid=(NZ // 2,),
             in_specs=[whole(NB, BLK, BLK)] + [pl.BlockSpec(memory_space=pltpu.HBM)] * len(pieces),
             out_specs=[whole(NX * BLK, HID), whole(NX * BLK, HID)],
             scratch_shapes=[
                 pltpu.VMEM((NZ, NY, BLK, HID), BF16),
                 pltpu.VMEM((nodes, HID), F32),
+                pltpu.VMEM((nodes, NY * BLK), BF16),
                 pltpu.VMEM((nodes, NY * BLK), BF16),
                 pltpu.SemaphoreType.DMA((len(pieces),)),
             ],
@@ -278,14 +291,12 @@
     gathered = [near_x, shift(near_x, "core", 1)]
 
     live = coords[0] >= 0
-    zr = lax.rem(coords[0] // NY - z + NZ, NZ)
     yr = lax.rem(coords[0] % NY - y + NY, NY)
     xr = lax.rem(coords[1] // NC - x + NX, NX)
     cr = lax.rem(coords[1] % NC - core + NC, NC)
-    forward_table = slot_table(zr * NY + yr, cr * NX + xr, live)
-    backward_table = slot_table(coords[0] // NY * NY + yr, cr * NX + xr, live)
-
-    y0, y1, y2, y3, zo = forward_blocks(forward_table, place, values, gathered)
+    table = slot_table(coords[0] // NY * NY + yr, cr * NX + xr, live)
+
+    y0, y1, y2, y3, zo = forward_blocks(table, values, gathered)
     values_t = turned(values, zo)
     by_y = ring_sum([y0, y1, y2, y3], "y").astype(BF16)
     by_z = exchange(zo, ZGROUPS)
@@ -320,7 +331,7 @@
     other = lax.dynamic_index_in_dim(shares, 1 - core, 1, keepdims=False)
     mine = mine + shift(other, "core", 1)
 
-    near, away = backward_blocks(backward_table, place, values_t, pieces)
+    near, away = backward_blocks(table, place, values_t, pieces)
     near = near + shift(away, "core", 1).astype(F32)
     spare = jnp.zeros((NX, 16 - mine.shape[1], HID), F32)
     both = jnp.concatenate([near.reshape(NX, BLK, HID), mine, spare], 1)

time: 200 us -> 199 us (level)
  no operation moved by 1% of the time
where the time goes in v3:
time: 199 us; the launch traced here: 198 us
  starting transfers between devices  79.5 us (40%)
  waiting for transfers between devices  77.4 us (39%)
  Pallas kernels  16.2 us (8%)
  local copies, waits for them, and re-layouts  13.3 us (7%)
  other arithmetic  8.17 us (4%)
  matrix products  2.28 us (1%)
    ppermute x15, waiting for transfers between devices, shift(): lax.ppermute(value, 'col', [(i, i // NY * NY + (i % NY + step) % NY) for...  34.1 us
    all_to_all x3, starting transfers between devices, exchange(): lax.all_to_all(parts, 'col', 0, 0, axis_index_groups=groups, tiled=True)  23.8 us
    ppermute x15, starting transfers between devices, shift(): lax.ppermute(value, 'col', [(i, i // NY * NY + (i % NY + step) % NY) for...  23.4 us
    ppermute x7, waiting for transfers between devices, shift(): lax.ppermute(value, 'row', [(i, (i // NC + step) % NX * NC + i % NC) for...  17.3 us
    all_to_all x3, waiting for transfers between devices, exchange(): lax.all_to_all(parts, 'col', 0, 0, axis_index_groups=groups, tiled=True)  14.8 us
    ppermute x7, starting transfers between devices, shift(): lax.ppermute(value, 'col', [(i, (i // NY + step) % NZ * NY + i % NY) for...  14.3 us
    all_to_all x1, starting transfers between devices, on_device(): shares = lax.all_to_all(local, 'col', 0, 0, tiled=True)  9.25 us
    unnamed x27, local copies, waits for them, and re-layouts  9.04 us
  transfers between devices with their start and end apart: 36, of which 21 were waited for; matrix products, arithmetic and copies ran while one was open for 4% of the time, Pallas kernels for 1%

profile of v3, /device:TPU:96, one launch (start us, length us, event | category | flops | bytes accessed | tf_op | source)
XLA Modules:
  0.0 198.0 jit_solution(4597781977312633538)
XLA Ops:
  4.9 3.2 %collective-permute-done.1 = bf16[128,512]{1,0:T(8,128)(2,1)S(1)} collective-permute-done((bf16[128,512]{1,0:T(8,128)(2,1)S(1)}, bf16[128,512]{1,0:T(8,128)(2,1)S(1)}, u32[]{:S(2)}, u32[]{:S(2)}) %collective-permute-start.1) | collective-permute-done | bytes 131104 | tf_op jit(solution)/shard_map/ppermute | solution.py:29
  8.4 5.9 %collective-permute-done.2 = bf16[128,512]{1,0:T(8,128)(2,1)S(1)} collective-permute-done((bf16[128,512]{1,0:T(8,128)(2,1)S(1)}, bf16[128,512]{1,0:T(8,128)(2,1)S(1)}, u32[]{:S(2)}, u32[]{:S(2)}) %collective-permute-start.2) | collective-permute-done | bytes 131104 | tf_op jit(solution)/shard_map/ppermute | solution.py:29
  18.2 6.8 %forward_blocks.1 = (bf16[8,96,512]{2,1,0:T(8,128)(2,1)S(1)}, bf16[8,96,512]{2,1,0:T(8,128)(2,1)S(1)}, bf16[8,96,512]{2,1,0:T(8,128)(2,1)S(1)}, bf16[8,96,512]{2,1,0:T(8,128)(2,1)S(1)}, bf16[8,4,32,512]{3,2,1,0:T(8,128)(2,1)}) custom-call(s32[256]{0:T(256)S(1)} %select_reduce_fusion.table, bf16[96,128,128]{2,1,0:T(8,128)(2,1)S(1)} %bitcast.96, ...), custom_call_target="tpu_custom_call" | custom-call | tf_op jit(solution)/shard_map/forward_blocks/pallas_call | solution.py:137
  28.9 7.7 %all-to-all-start.1 = ((bf16[8,4,32,512]{3,2,1,0:T(8,128)(2,1)}), bf16[8,4,32,512]{3,2,1,0:T(8,128)(2,1)}, u32[]{:S(2)}, u32[]{:S(2)}) async-start(bf16[8,4,32,512]{3,2,1,0:T(8,128)(2,1)} %get-tuple-element.14.after), calls=%async_computation.1 | async-start | bytes 2097152 | tf_op jit(solution)/shard_map/all_to_all | solution.py:274
  39.1 3.8 %collective-permute-start.7 = (bf16[8,96,512]{2,1,0:T(8,128)(2,1)S(1)}, bf16[8,96,512]{2,1,0:T(8,128)(2,1)S(1)}, u32[]{:S(2)}, u32[]{:S(2)}) collective-permute-start(bf16[8,96,512]{2,1,0:T(8,128)(2,1)S(1)} %pad_maximum_fusion.1), channel_id=1, source_target_pairs={{0,3},{1,0},{2,1},{3,2},{4,7},{5,4},{6,5},{7,6},{8,11},{9,8},{10,9... | collective-permute-start | bytes 2359304 | tf_op jit(solution)/shard_map/ppermute | solution.py:25
  44.1 15.0 %collective-permute-done.7 = bf16[8,96,512]{2,1,0:T(8,128)(2,1)S(1)} collective-permute-done((bf16[8,96,512]{2,1,0:T(8,128)(2,1)S(1)}, bf16[8,96,512]{2,1,0:T(8,128)(2,1)S(1)}, u32[]{:S(2)}, u32[]{:S(2)}) %collective-permute-start.7) | collective-permute-done | bytes 786464 | tf_op jit(solution)/shard_map/ppermute | solution.py:25
  59.1 4.7 %collective-permute-done.5 = bf16[8,96,512]{2,1,0:T(8,128)(2,1)S(1)} collective-permute-done((bf16[8,96,512]{2,1,0:T(8,128)(2,1)S(1)}, bf16[8,96,512]{2,1,0:T(8,128)(2,1)S(1)}, u32[]{:S(2)}, u32[]{:S(2)}) %collective-permute-start.5) | collective-permute-done | bytes 786464 | tf_op jit(solution)/shard_map/ppermute | solution.py:25
  65.0 7.7 %all-to-all-start = ((bf16[8,96,512]{2,1,0:T(8,128)(2,1)}), bf16[8,96,512]{2,1,0:T(8,128)(2,1)S(1)}, u32[]{:S(2)}, u32[]{:S(2)}) async-start(bf16[8,96,512]{2,1,0:T(8,128)(2,1)} %add_convert_fusion), calls=%async_computation | async-start | bytes 1572864 | tf_op jit(solution)/shard_map/all_to_all | solution.py:274
  74.2 3.2 %collective-permute-start.10 = (f32[16,512]{1,0:T(8,128)S(1)}, f32[16,512]{1,0:T(8,128)S(1)}, u32[]{:S(2)}, u32[]{:S(2)}) collective-permute-start(f32[16,512]{1,0:T(8,128)S(1)} %get-tuple-element.28), channel_id=1, source_target_pairs={{0,3},{1,0},{2,1},{3,2},{4,7},{5,4},{6,5},{7,6},{8,11},{9,8},{10,9... | collective-permute-start | bytes 98312 | tf_op jit(solution)/shard_map/ppermute | solution.py:25
  79.3 3.3 %collective-permute-start.11 = (f32[32,512]{1,0:T(8,128)S(1)}, f32[32,512]{1,0:T(8,128)S(1)}, u32[]{:S(2)}, u32[]{:S(2)}) collective-permute-start(f32[32,512]{1,0:T(8,128)S(1)} %pad_maximum_fusion.8), channel_id=1, source_target_pairs={{0,3},{1,0},{2,1},{3,2},{4,7},{5,4},{6,5},{7,6},{8,11},{9,8},{10,9... | collective-permute-start | bytes 196616 | tf_op jit(solution)/shard_map/ppermute | solution.py:25
  84.5 3.6 %collective-permute-done.9 = f32[32,512]{1,0:T(8,128)S(1)} collective-permute-done((f32[32,512]{1,0:T(8,128)S(1)}, f32[32,512]{1,0:T(8,128)S(1)}, u32[]{:S(2)}, u32[]{:S(2)}) %collective-permute-start.9) | collective-permute-done | bytes 65568 | tf_op jit(solution)/shard_map/ppermute | solution.py:25
  92.1 8.4 %all-to-all-start.2 = ((bf16[8,80,512]{2,1,0:T(8,128)(2,1)}), bf16[8,80,512]{2,1,0:T(8,128)(2,1)}, u32[]{:S(2)}, u32[]{:S(2)}) async-start(bf16[8,80,512]{2,1,0:T(8,128)(2,1)} %broadcast_in_dim.14), calls=%async_computation.2 | async-start | bytes 1310720 | tf_op jit(solution)/shard_map/all_to_all | solution.py:274
  101.8 13.2 %all-to-all-done.2.rest_0_ = bf16[8,80,512]{2,1,0:T(8,128)(2,1)} async-done(((bf16[8,80,512]{2,1,0:T(8,128)(2,1)}), bf16[8,80,512]{2,1,0:T(8,128)(2,1)}, u32[]{:S(2)}, u32[]{:S(2)}) %all-to-all-start.2) | async-done | bytes 655392 | tf_op jit(solution)/shard_map/all_to_all | solution.py:274
  115.0 9.2 %all-to-all-start.3 = ((bf16[32,16,512]{2,1,0:T(8,128)(2,1)}), bf16[32,16,512]{2,1,0:T(8,128)(2,1)}, u32[]{:S(2)}, u32[]{:S(2)}) async-start(bf16[32,16,512]{2,1,0:T(8,128)(2,1)} %bitcast.98), calls=%async_computation.3 | async-start | bytes 1048576 | tf_op jit(solution)/shard_map/all_to_all | solution.py:326
  133.6 3.2 %collective-permute-done.18 = bf16[48,512]{1,0:T(8,128)(2,1)S(1)} collective-permute-done((bf16[48,512]{1,0:T(8,128)(2,1)S(1)}, bf16[48,512]{1,0:T(8,128)(2,1)S(1)}, u32[]{:S(2)}, u32[]{:S(2)}) %collective-permute-start.18) | collective-permute-done | bytes 49184 | tf_op jit(solution)/shard_map/ppermute | solution.py:25
  136.8 3.6 %collective-permute-start.22 = (bf16[4,48,512]{2,1,0:T(8,128)(2,1)S(1)}, bf16[4,48,512]{2,1,0:T(8,128)(2,1)S(1)}, u32[]{:S(2)}, u32[]{:S(2)}) collective-permute-start(bf16[4,48,512]{2,1,0:T(8,128)(2,1)S(1)} %pad_maximum_fusion.4.rest_5_), channel_id=1, source_target_pairs={{0,4},{1,5},{2,6},{3,7},{4,8},{5,9},{6,10},{7,11},{8,12},{9,13},{1... | collective-permute-start | bytes 589832 | tf_op jit(solution)/shard_map/ppermute | solution.py:21
  140.4 3.8 %collective-permute-done.22.rest_12_ = bf16[4,48,512]{2,1,0:T(8,128)(2,1)S(1)} collective-permute-done((bf16[4,48,512]{2,1,0:T(8,128)(2,1)S(1)}, bf16[4,48,512]{2,1,0:T(8,128)(2,1)S(1)}, u32[]{:S(2)}, u32[]{:S(2)}) %collective-permute-start.22) | collective-permute-done | bytes 196640 | tf_op jit(solution)/shard_map/ppermute | solution.py:21
  144.3 3.7 %collective-permute-start.23 = (bf16[4,48,512]{2,1,0:T(8,128)(2,1)S(1)}, bf16[4,48,512]{2,1,0:T(8,128)(2,1)}, u32[]{:S(2)}, u32[]{:S(2)}) collective-permute-start(bf16[4,48,512]{2,1,0:T(8,128)(2,1)S(1)} %collective-permute-done.22.rest_12_), channel_id=1, source_target_pairs={{0,4},{1,5},{2,6},{3,7},{4,8},{5,9},{6,10},{7,11},{8,12},{9,13},{1... | collective-permute-start | bytes 589832 | tf_op jit(solution)/shard_map/ppermute | solution.py:21
  148.1 4.3 %collective-permute-done.23.rest_11_ = bf16[4,48,512]{2,1,0:T(8,128)(2,1)} collective-permute-done((bf16[4,48,512]{2,1,0:T(8,128)(2,1)S(1)}, bf16[4,48,512]{2,1,0:T(8,128)(2,1)}, u32[]{:S(2)}, u32[]{:S(2)}) %collective-permute-start.23) | collective-permute-done | bytes 196640 | tf_op jit(solution)/shard_map/ppermute | solution.py:21
  152.4 3.8 %collective-permute-start.24 = (bf16[4,48,512]{2,1,0:T(8,128)(2,1)}, bf16[4,48,512]{2,1,0:T(8,128)(2,1)}, u32[]{:S(2)}, u32[]{:S(2)}) collective-permute-start(bf16[4,48,512]{2,1,0:T(8,128)(2,1)} %collective-permute-done.23.rest_11_), channel_id=1, source_target_pairs={{0,4},{1,5},{2,6},{3,7},{4,8},{5,9},{6,10},{7,11},{8,12},{9,13},{1... | collective-permute-start | bytes 589832 | tf_op jit(solution)/shard_map/ppermute | solution.py:21
  159.5 3.2 %collective-permute-start.15 = (bf16[4,80,512]{2,1,0:T(8,128)(2,1)}, bf16[4,80,512]{2,1,0:T(8,128)(2,1)}, u32[]{:S(2)}, u32[]{:S(2)}) collective-permute-start(bf16[4,80,512]{2,1,0:T(8,128)(2,1)} %slice.204), channel_id=1, source_target_pairs={{0,3},{1,0},{2,1},{3,2},{4,7},{5,4},{6,5},{7,6},{8,11},{9,8},{10,9... | collective-permute-start | bytes 983048 | tf_op jit(solution)/shard_map/ppermute | solution.py:25
  162.7 3.2 %collective-permute-start.25 = (bf16[4,48,512]{2,1,0:T(8,128)(2,1)}, bf16[4,48,512]{2,1,0:T(8,128)(2,1)}, u32[]{:S(2)}, u32[]{:S(2)}) collective-permute-start(bf16[4,48,512]{2,1,0:T(8,128)(2,1)} %collective-permute-done.24.rest_10_), channel_id=1, source_target_pairs={{0,4},{1,5},{2,6},{3,7},{4,8},{5,9},{6,10},{7,11},{8,12},{9,13},{1... | collective-permute-start | bytes 589832 | tf_op jit(solution)/shard_map/ppermute | solution.py:21
  173.4 7.6 %backward_blocks.1 = (f32[512,512]{1,0:T(8,128)S(1)}, bf16[512,512]{1,0:T(8,128)(2,1)S(1)}) custom-call(s32[256]{0:T(256)S(1)} %select_reduce_fusion.table, s32[2]{0:T(128)S(1)} %pad_add_fusion.place, bf16[96,128,128]{2,1,0:T(8,128)(2,1)S(1)} %copy-done.3, bf16[8,80,512]{2,1,0:T(8,128)(2,1)} %all-to-all-done.2.rest_0_, bf16[8,80,512]{2,1,0:T(8,128)(2,1)S(1)} %copy-done.8, ...), custom_call_target="tpu_custom_call" | custom-call | tf_op jit(solution)/shard_map/backward_blocks/pallas_call | solution.py:222
  193.2 3.0 %collective-permute-done.29 = bf16[144,512]{1,0:T(8,128)(2,1)S(1)} collective-permute-done((bf16[144,512]{1,0:T(8,128)(2,1)S(1)}, bf16[144,512]{1,0:T(8,128)(2,1)S(1)}, u32[]{:S(2)}, u32[]{:S(2)}) %collective-permute-start.29) | collective-permute-done | bytes 147488 | tf_op jit(solution)/shard_map/ppermute | solution.py:29
  (132 shorter events, 61.8 us)
Async XLA Ops:
  1.6 6.5 %collective-permute-start.1 = (bf16[128,512]{1,0:T(8,128)(2,1)S(1)}, bf16[128,512]{1,0:T(8,128)(2,1)S(1)}, u32[]{:S(2)}, u32[]{:S(2)}) collective-permute-start(bf16[128,512]{1,0:T(8,128)(2,1)S(1)} %convert_element_type.78), channel_id=1, source_target_pairs={{0,64},{32,96},{64,128},{96,160},{128,192},{160,224},{192,0},{224,... | collective-permute-start | bytes 393224 | tf_op jit(solution)/shard_map/ppermute | solution.py:29
  8.1 6.2 %collective-permute-start.2 = (bf16[128,512]{1,0:T(8,128)(2,1)S(1)}, bf16[128,512]{1,0:T(8,128)(2,1)S(1)}, u32[]{:S(2)}, u32[]{:S(2)}) collective-permute-start(bf16[128,512]{1,0:T(8,128)(2,1)S(1)} %collective-permute-done.1), channel_id=1, source_target_pairs={{0,64},{32,96},{64,128},{96,160},{128,192},{160,224},{192,0},{224,... | collective-permute-start | bytes 393224 | tf_op jit(solution)/shard_map/ppermute | solution.py:29
  25.9 12.0 %collective-permute-start.6 = (bf16[4,96,512]{2,1,0:T(8,128)(2,1)}, bf16[4,96,512]{2,1,0:T(8,128)(2,1)}, u32[]{:S(2)}, u32[]{:S(2)}) collective-permute-start(bf16[4,96,512]{2,1,0:T(8,128)(2,1)} %get-tuple-element.18), channel_id=1, source_target_pairs={{0,3},{1,0},{2,1},{3,2},{4,7},{5,4},{6,5},{7,6},{8,11},{9,8},{10,9... | collective-permute-start | bytes 1179656 | tf_op jit(solution)/shard_map/ppermute | solution.py:25
  28.9 13.9 %collective-permute-start.4 = (bf16[4,96,512]{2,1,0:T(8,128)(2,1)S(1)}, bf16[4,96,512]{2,1,0:T(8,128)(2,1)}, u32[]{:S(2)}, u32[]{:S(2)}) collective-permute-start(bf16[4,96,512]{2,1,0:T(8,128)(2,1)S(1)} %get-tuple-element.17), channel_id=1, source_target_pairs={{0,1},{1,2},{2,3},{3,0},{4,5},{5,6},{6,7},{7,4},{8,9},{9,10},{10,1... | collective-permute-start | bytes 1179656 | tf_op jit(solution)/shard_map/ppermute | solution.py:25
  28.9 36.1 %all-to-all-start.1 = ((bf16[8,4,32,512]{3,2,1,0:T(8,128)(2,1)}), bf16[8,4,32,512]{3,2,1,0:T(8,128)(2,1)}, u32[]{:S(2)}, u32[]{:S(2)}) async-start(bf16[8,4,32,512]{3,2,1,0:T(8,128)(2,1)} %get-tuple-element.14.after), calls=%async_computation.1 | async-start | bytes 2097152 | tf_op jit(solution)/shard_map/all_to_all | solution.py:274
  39.1 20.0 %collective-permute-start.7 = (bf16[8,96,512]{2,1,0:T(8,128)(2,1)S(1)}, bf16[8,96,512]{2,1,0:T(8,128)(2,1)S(1)}, u32[]{:S(2)}, u32[]{:S(2)}) collective-permute-start(bf16[8,96,512]{2,1,0:T(8,128)(2,1)S(1)} %pad_maximum_fusion.1), channel_id=1, source_target_pairs={{0,3},{1,0},{2,1},{3,2},{4,7},{5,4},{6,5},{7,6},{8,11},{9,8},{10,9... | collective-permute-start | bytes 2359304 | tf_op jit(solution)/shard_map/ppermute | solution.py:25
  44.0 19.7 %collective-permute-start.5 = (bf16[8,96,512]{2,1,0:T(8,128)(2,1)S(1)}, bf16[8,96,512]{2,1,0:T(8,128)(2,1)S(1)}, u32[]{:S(2)}, u32[]{:S(2)}) collective-permute-start(bf16[8,96,512]{2,1,0:T(8,128)(2,1)S(1)} %pad_maximum_fusion), channel_id=1, source_target_pairs={{0,1},{1,2},{2,3},{3,0},{4,5},{5,6},{6,7},{7,4},{8,9},{9,10},{10,1... | collective-permute-start | bytes 2359304 | tf_op jit(solution)/shard_map/ppermute | solution.py:25
  65.0 24.8 %all-to-all-start = ((bf16[8,96,512]{2,1,0:T(8,128)(2,1)}), bf16[8,96,512]{2,1,0:T(8,128)(2,1)S(1)}, u32[]{:S(2)}, u32[]{:S(2)}) async-start(bf16[8,96,512]{2,1,0:T(8,128)(2,1)} %add_convert_fusion), calls=%async_computation | async-start | bytes 1572864 | tf_op jit(solution)/shard_map/all_to_all | solution.py:274
  92.1 22.9 %all-to-all-start.2 = ((bf16[8,80,512]{2,1,0:T(8,128)(2,1)}), bf16[8,80,512]{2,1,0:T(8,128)(2,1)}, u32[]{:S(2)}, u32[]{:S(2)}) async-start(bf16[8,80,512]{2,1,0:T(8,128)(2,1)} %broadcast_in_dim.14), calls=%async_computation.2 | async-start | bytes 1310720 | tf_op jit(solution)/shard_map/all_to_all | solution.py:274
  115.0 54.0 %all-to-all-start.3 = ((bf16[32,16,512]{2,1,0:T(8,128)(2,1)}), bf16[32,16,512]{2,1,0:T(8,128)(2,1)}, u32[]{:S(2)}, u32[]{:S(2)}) async-start(bf16[32,16,512]{2,1,0:T(8,128)(2,1)} %bitcast.98), calls=%async_computation.3 | async-start | bytes 1048576 | tf_op jit(solution)/shard_map/all_to_all | solution.py:326
  125.8 7.8 %collective-permute-start.16 = (bf16[48,512]{1,0:T(8,128)(2,1)S(1)}, bf16[48,512]{1,0:T(8,128)(2,1)S(1)}, u32[]{:S(2)}, u32[]{:S(2)}) collective-permute-start(bf16[48,512]{1,0:T(8,128)(2,1)S(1)} %get-tuple-element.32), channel_id=1, source_target_pairs={{0,3},{1,0},{2,1},{3,2},{4,7},{5,4},{6,5},{7,6},{8,11},{9,8},{10,9... | collective-permute-start | bytes 147464 | tf_op jit(solution)/shard_map/ppermute | solution.py:25
  130.2 6.6 %collective-permute-start.18 = (bf16[48,512]{1,0:T(8,128)(2,1)S(1)}, bf16[48,512]{1,0:T(8,128)(2,1)S(1)}, u32[]{:S(2)}, u32[]{:S(2)}) collective-permute-start(bf16[48,512]{1,0:T(8,128)(2,1)S(1)} %collective-permute-done.17), channel_id=1, source_target_pairs={{0,1},{1,2},{2,3},{3,0},{4,5},{5,6},{6,7},{7,4},{8,9},{9,10},{10,1... | collective-permute-start | bytes 147464 | tf_op jit(solution)/shard_map/ppermute | solution.py:25
  130.4 25.9 %collective-permute-start.13 = (bf16[8,80,512]{2,1,0:T(8,128)(2,1)}, bf16[8,80,512]{2,1,0:T(8,128)(2,1)S(1)}, u32[]{:S(2)}, u32[]{:S(2)}) collective-permute-start(bf16[8,80,512]{2,1,0:T(8,128)(2,1)} %all-to-all-done.2.rest_0_), channel_id=1, source_target_pairs={{0,1},{1,2},{2,3},{3,0},{4,5},{5,6},{6,7},{7,4},{8,9},{9,10},{10,1... | collective-permute-start | bytes 1966088 | tf_op jit(solution)/shard_map/ppermute | solution.py:25
  132.0 25.8 %collective-permute-start.12 = (bf16[8,80,512]{2,1,0:T(8,128)(2,1)}, bf16[8,80,512]{2,1,0:T(8,128)(2,1)S(1)}, u32[]{:S(2)}, u32[]{:S(2)}) collective-permute-start(bf16[8,80,512]{2,1,0:T(8,128)(2,1)} %all-to-all-done.2.rest_0_), channel_id=1, source_target_pairs={{0,3},{1,0},{2,1},{3,2},{4,7},{5,4},{6,5},{7,6},{8,11},{9,8},{10,9... | collective-permute-start | bytes 1966088 | tf_op jit(solution)/shard_map/ppermute | solution.py:25
  136.8 7.4 %collective-permute-start.22 = (bf16[4,48,512]{2,1,0:T(8,128)(2,1)S(1)}, bf16[4,48,512]{2,1,0:T(8,128)(2,1)S(1)}, u32[]{:S(2)}, u32[]{:S(2)}) collective-permute-start(bf16[4,48,512]{2,1,0:T(8,128)(2,1)S(1)} %pad_maximum_fusion.4.rest_5_), channel_id=1, source_target_pairs={{0,4},{1,5},{2,6},{3,7},{4,8},{5,9},{6,10},{7,11},{8,12},{9,13},{1... | collective-permute-start | bytes 589832 | tf_op jit(solution)/shard_map/ppermute | solution.py:21
  140.4 7.7 %collective-permute-start.19 = (bf16[4,48,512]{2,1,0:T(8,128)(2,1)S(1)}, bf16[4,48,512]{2,1,0:T(8,128)(2,1)}, u32[]{:S(2)}, u32[]{:S(2)}) collective-permute-start(bf16[4,48,512]{2,1,0:T(8,128)(2,1)S(1)} %pad_maximum_fusion.4.rest_5_), channel_id=1, source_target_pairs={{0,28},{1,29},{2,30},{3,31},{4,0},{5,1},{6,2},{7,3},{8,4},{9,5},{1... | collective-permute-start | bytes 589832 | tf_op jit(solution)/shard_map/ppermute | solution.py:21
  144.3 8.2 %collective-permute-start.23 = (bf16[4,48,512]{2,1,0:T(8,128)(2,1)S(1)}, bf16[4,48,512]{2,1,0:T(8,128)(2,1)}, u32[]{:S(2)}, u32[]{:S(2)}) collective-permute-start(bf16[4,48,512]{2,1,0:T(8,128)(2,1)S(1)} %collective-permute-done.22.rest_12_), channel_id=1, source_target_pairs={{0,4},{1,5},{2,6},{3,7},{4,8},{5,9},{6,10},{7,11},{8,12},{9,13},{1... | collective-permute-start | bytes 589832 | tf_op jit(solution)/shard_map/ppermute | solution.py:21
  148.1 14.6 %collective-permute-start.20 = (bf16[4,48,512]{2,1,0:T(8,128)(2,1)}, bf16[4,48,512]{2,1,0:T(8,128)(2,1)}, u32[]{:S(2)}, u32[]{:S(2)}) collective-permute-start(bf16[4,48,512]{2,1,0:T(8,128)(2,1)} %collective-permute-done.19.rest_6_), channel_id=1, source_target_pairs={{0,28},{1,29},{2,30},{3,31},{4,0},{5,1},{6,2},{7,3},{8,4},{9,5},{1... | collective-permute-start | bytes 589832 | tf_op jit(solution)/shard_map/ppermute | solution.py:21
  152.4 10.3 %collective-permute-start.24 = (bf16[4,48,512]{2,1,0:T(8,128)(2,1)}, bf16[4,48,512]{2,1,0:T(8,128)(2,1)}, u32[]{:S(2)}, u32[]{:S(2)}) collective-permute-start(bf16[4,48,512]{2,1,0:T(8,128)(2,1)} %collective-permute-done.23.rest_11_), channel_id=1, source_target_pairs={{0,4},{1,5},{2,6},{3,7},{4,8},{5,9},{6,10},{7,11},{8,12},{9,13},{1... | collective-permute-start | bytes 589832 | tf_op jit(solution)/shard_map/ppermute | solution.py:21
  157.8 12.6 %collective-permute-start.14 = (bf16[4,80,512]{2,1,0:T(8,128)(2,1)}, bf16[4,80,512]{2,1,0:T(8,128)(2,1)}, u32[]{:S(2)}, u32[]{:S(2)}) collective-permute-start(bf16[4,80,512]{2,1,0:T(8,128)(2,1)} %slice.203), channel_id=1, source_target_pairs={{0,1},{1,2},{2,3},{3,0},{4,5},{5,6},{6,7},{7,4},{8,9},{9,10},{10,1... | collective-permute-start | bytes 983048 | tf_op jit(solution)/shard_map/ppermute | solution.py:25
  159.5 11.0 %collective-permute-start.15 = (bf16[4,80,512]{2,1,0:T(8,128)(2,1)}, bf16[4,80,512]{2,1,0:T(8,128)(2,1)}, u32[]{:S(2)}, u32[]{:S(2)}) collective-permute-start(bf16[4,80,512]{2,1,0:T(8,128)(2,1)} %slice.204), channel_id=1, source_target_pairs={{0,3},{1,0},{2,1},{3,2},{4,7},{5,4},{6,5},{7,6},{8,11},{9,8},{10,9... | collective-permute-start | bytes 983048 | tf_op jit(solution)/shard_map/ppermute | solution.py:25
  162.7 7.7 %collective-permute-start.21 = (bf16[4,48,512]{2,1,0:T(8,128)(2,1)}, bf16[4,48,512]{2,1,0:T(8,128)(2,1)}, u32[]{:S(2)}, u32[]{:S(2)}) collective-permute-start(bf16[4,48,512]{2,1,0:T(8,128)(2,1)} %collective-permute-done.20.rest_7_), channel_id=1, source_target_pairs={{0,28},{1,29},{2,30},{3,31},{4,0},{5,1},{6,2},{7,3},{8,4},{9,5},{1... | collective-permute-start | bytes 589832 | tf_op jit(solution)/shard_map/ppermute | solution.py:21
  162.7 7.7 %collective-permute-start.25 = (bf16[4,48,512]{2,1,0:T(8,128)(2,1)}, bf16[4,48,512]{2,1,0:T(8,128)(2,1)}, u32[]{:S(2)}, u32[]{:S(2)}) collective-permute-start(bf16[4,48,512]{2,1,0:T(8,128)(2,1)} %collective-permute-done.24.rest_10_), channel_id=1, source_target_pairs={{0,4},{1,5},{2,6},{3,7},{4,8},{5,9},{6,10},{7,11},{8,12},{9,13},{1... | collective-permute-start | bytes 589832 | tf_op jit(solution)/shard_map/ppermute | solution.py:21
  189.8 6.4 %collective-permute-start.29 = (bf16[144,512]{1,0:T(8,128)(2,1)S(1)}, bf16[144,512]{1,0:T(8,128)(2,1)S(1)}, u32[]{:S(2)}, u32[]{:S(2)}) collective-permute-start(bf16[144,512]{1,0:T(8,128)(2,1)S(1)} %pad_maximum_fusion.5), channel_id=1, source_target_pairs={{0,64},{32,96},{64,128},{96,160},{128,192},{160,224},{192,0},{224,... | collective-permute-start | bytes 442376 | tf_op jit(solution)/shard_map/ppermute | solution.py:29
  (25 other events, 173.8 us)
